TPU v7x, 256 devices: a whole 4x4x8 slice. The times are simulated.
256 devices in a mesh: tile: 32 (over y, z), freq: 8 (over x, core).
Axes of the slice: x: 4, y: 4, z: 8, core: 2. Of those that a mesh axis runs over, the one named last changes fastest.
Arguments:
- visibilities: float32 [8, 4096, 2, 128], P('freq', 'tile'), may hold values from -6 to 6
- uv_cell: int32 [8, 4096, 2, 128], P('freq', 'tile'), may hold values from 0 to 120
- sub_pixel: int32 [8, 4096, 2, 128], P('freq', 'tile'), may hold values from 0 to 7
- w_plane: int32 [8, 4096], P('freq', 'tile'), may hold values from 0 to 15
- block_tile: int32 [8, 4096], P('freq', 'tile'), may hold values from 0 to 63, as said below
- model_grid: bfloat16 [8, 64, 128, 256], P('freq', 'tile'), may hold values from -3 to 3
- kernel_table: bfloat16 [16, 8, 8], replicated, may hold values from 0.049804688 to 1
- coupling: float32 [8, 8], replicated, may hold values from -2 to 2
Outputs:
- residuals: float32 [8, 4096, 2, 128], P('freq', 'tile')
- coupled_grid: float32 [8, 64, 128, 256], P('freq', 'tile')
Inputs may be any that keep to these rules, and one draw needn't show every extreme that they name: `block_tile`: among the 128 blocks of one plane on one device (aligned blocks), at most 12 have tiles of one owner, the owner of tile k being k // 2; in every plane some owner gets exactly 12 blocks from every device.
All inputs are finite; a program needn't handle non-finite values.
Results may differ from a plain program's by a relative error of at most 0.0034.
Values may be sent and summed in bfloat16 or wider, within the bound.
A program may use at most 64 MiB of HBM per device.

v0:
```python
import jax
import jax.numpy as jnp
from jax import lax
from jax.sharding import PartitionSpec as P


def lookup_taps(index, table_flat):
    entries = table_flat.shape[0]
    picks = (index[:, :, None] == jnp.arange(entries, dtype=jnp.int32)[None, None, :]).astype(
        jnp.bfloat16
    )
    return jnp.einsum("brk,ks->bsr", picks, table_flat, preferred_element_type=jnp.float32).astype(
        jnp.bfloat16
    )


def place_slots(values, slot, total, filler):
    empty = jnp.full((total,) + values.shape[1:], filler, values.dtype)
    return empty.at[slot].set(values)


def spread_taps(taps, start, side):
    columns = jnp.arange(side, dtype=jnp.int32)
    offset = columns[None, None, :] - start[:, :, None]
    matrix = jnp.zeros(offset.shape, jnp.bfloat16)
    for which in range(taps.shape[1]):
        matrix = matrix + jnp.where(
            offset == which, taps[:, which, :, None], jnp.zeros((), jnp.bfloat16)
        )
    return matrix


def grid_slots(samples, taps_row, taps_column, position, tile_slot, model_tiles):
    tiles_here = model_tiles.shape[0]
    side = model_tiles.shape[1]
    total = samples.shape[0]
    turns = 6
    cluster_count = total // turns

    def advance(grid_sum, pieces):
        sample_part, row_part, column_part, position_part, tile_part = pieces
        row_matrix = spread_taps(row_part, position_part // side, side)
        column_matrix = spread_taps(column_part, position_part % side, side).astype(jnp.float32)
        chosen = jnp.take(model_tiles, tile_part, axis=0)
        partial_value = jnp.einsum(
            "gri,gij->grj", row_matrix, chosen, preferred_element_type=jnp.float32
        )
        model_real = jnp.sum(partial_value[:, :, :side] * column_matrix, axis=2)
        model_imag = jnp.sum(partial_value[:, :, side:] * column_matrix, axis=2)
        residual = sample_part - jnp.stack([model_real, model_imag], axis=1)
        weighted = jnp.concatenate(
            [residual[:, 0, :, None] * column_matrix, residual[:, 1, :, None] * column_matrix],
            axis=2,
        ).astype(jnp.bfloat16)
        selector = tile_part[:, None] == jnp.arange(tiles_here, dtype=jnp.int32)[None, :]
        masked_rows = jnp.where(
            selector[:, :, None, None], row_matrix[:, None, :, :], jnp.zeros((), jnp.bfloat16)
        )
        grid_sum = grid_sum + jnp.einsum(
            "gtri,grj->tij", masked_rows, weighted, preferred_element_type=jnp.float32
        )
        return (grid_sum, residual)

    def split(values):
        return values.reshape((turns, cluster_count) + values.shape[1:])

    start_grid = jnp.zeros((tiles_here, side, 2 * side), jnp.float32)
    grid_sum, residual = lax.scan(
        advance,
        start_grid,
        (split(samples), split(taps_row), split(taps_column), split(position), split(tile_slot)),
    )
    return (grid_sum, residual.reshape(samples.shape))


def body(visibilities, uv_cell, sub_pixel, w_plane, block_tile, model_grid, kernel_table, coupling):
    blocks = visibilities.shape[1]
    rows = visibilities.shape[3]
    owners = lax.axis_size("tile")
    capacity = 3 * blocks // owners
    total = owners * capacity
    tiles_here = model_grid.shape[1]
    side = model_grid.shape[2]
    kernel_planes = kernel_table.shape[0]
    oversample = kernel_table.shape[1]
    support = kernel_table.shape[2]
    table_flat = kernel_table.reshape(kernel_planes * oversample, support)
    samples = visibilities[0]
    cells = uv_cell[0]
    offsets = sub_pixel[0]
    plane_of = w_plane[0]
    tile_id = block_tile[0]
    owner = tile_id // tiles_here
    local_tile = tile_id % tiles_here
    member = (owner[:, None] == jnp.arange(owners, dtype=jnp.int32)[None, :]).astype(jnp.int32)
    rank = jnp.sum(jnp.cumsum(member, axis=0) * member, axis=1) - 1
    slot = owner * capacity + rank
    position = cells[:, 0, :] * side + cells[:, 1, :]
    sent_samples = place_slots(samples, slot, total, 0.0).reshape(owners, capacity, 2, rows)

    def flatten(values):
        return values.reshape((total,) + values.shape[2:])

    taps = jnp.concatenate(
        [
            lookup_taps(plane_of[:, None] * oversample + offsets[:, 0, :], table_flat),
            lookup_taps(plane_of[:, None] * oversample + offsets[:, 1, :], table_flat),
        ],
        axis=1,
    )
    sent_position = place_slots(position, slot, total, 0).reshape(owners, capacity, rows)
    sent_tile = place_slots(local_tile, slot, total, 0).reshape(owners, capacity)
    got_samples, got_position, got_tile = (
        lax.all_to_all(sent_samples, "tile", split_axis=0, concat_axis=0, tiled=True),
        lax.all_to_all(sent_position, "tile", split_axis=0, concat_axis=0, tiled=True),
        lax.all_to_all(sent_tile, "tile", split_axis=0, concat_axis=0, tiled=True),
    )
    sent_taps = place_slots(taps, slot, total, 0.0).reshape(owners, capacity, 2 * support, rows)
    got_taps = flatten(lax.all_to_all(sent_taps, "tile", split_axis=0, concat_axis=0, tiled=True))
    got_samples = flatten(got_samples)
    got_position = flatten(got_position)
    got_tile = flatten(got_tile)
    taps_row = got_taps[:, :support]
    taps_column = got_taps[:, support:]
    grid_sum, residual = grid_slots(
        got_samples, taps_row, taps_column, got_position, got_tile, model_grid[0]
    )
    returned = lax.all_to_all(
        residual.reshape(owners, capacity, 2, rows), "tile", split_axis=0, concat_axis=0, tiled=True
    )
    residuals = jnp.take(flatten(returned), slot, axis=0)[None]
    grid_rounded = grid_sum.astype(jnp.bfloat16)[None]
    plane_index = lax.axis_index("freq")
    own_row = lax.dynamic_index_in_dim(coupling, plane_index, 0, keepdims=False)
    coupled_grid = jnp.sum(
        own_row[:, None, None, None]
        * lax.all_gather(grid_rounded, "freq", axis=0, tiled=True).astype(jnp.float32),
        axis=0,
    )[None]
    return (residuals, coupled_grid)


def solution(mesh):
    return jax.shard_map(
        body,
        mesh=mesh,
        in_specs=(
            P("freq", "tile", None, None),
            P("freq", "tile", None, None),
            P("freq", "tile", None, None),
            P("freq", "tile"),
            P("freq", "tile"),
            P("freq", "tile", None, None),
            P(),
            P(),
        ),
        out_specs=(P("freq", "tile", None, None), P("freq", "tile", None, None)),
        check_vma=False,
    )
```

profile of v0, /device:TPU:1, one launch (start us, length us, event | category | flops | bytes accessed | tf_op | source)
XLA Modules:
  0.0 572.8 jit_solution(3414338093599745116)
XLA Ops:
  10.7 12.0 %all-to-all-start = ((s32[32,1,12]{2,1,0:T(1,128)}), s32[32,1,12]{2,1,0:T(1,128)S(1)}, u32[]{:S(2)}, u32[]{:S(2)}) async-start(s32[32,1,12]{2,1,0:T(1,128)} %bitcast.4), calls=%async_computation | async-start | bytes 32768 | tf_op jit(solution)/shard_map/all_to_all | solution.py:116
  22.7 1.1 fusion.93
  24.5 1.1 slice_add_fusion
  28.2 3.1 all-to-all-done
  31.3 6.2 %all-to-all-start.1 = ((s32[32,12,128]{2,1,0:T(8,128)}), s32[32,12,128]{2,1,0:T(8,128)S(1)}, u32[]{:S(2)}, u32[]{:S(2)}) async-start(s32[32,12,128]{2,1,0:T(8,128)} %reshape.378), calls=%async_computation.1 | async-start | bytes 524288 | tf_op jit(solution)/shard_map/all_to_all | solution.py:115
  37.4 3.7 fusion.83
  41.1 3.7 fusion.84
  44.9 1.4 broadcast_in_dim.341
  46.3 12.4 %scatter_fusion = bf16[384,16,128]{2,1,0:T(8,128)(2,1)} fusion(bf16[384,16,128]{2,1,0:T(8,128)(2,1)} %broadcast_in_dim.341, s32[128]{0:T(128)S(1)} %fusion.90, bf16[128,16,128]{2,1,0:T(8,128)(2,1)S(1)} %pad_maximum_fusion), kind=kCustom, calls=%fused_computation.4 | custom fusion | bytes 1573376 | tf_op jit(solution)/shard_map/scatter | solution.py:19
  58.7 9.4 %all-to-all-start.2 = ((bf16[32,12,16,128]{3,2,1,0:T(8,128)(2,1)}), bf16[32,12,16,128]{3,2,1,0:T(8,128)(2,1)S(1)}, u32[]{:S(2)}, u32[]{:S(2)}) async-start(bf16[32,12,16,128]{3,2,1,0:T(8,128)(2,1)} %bitcast.13), calls=%async_computation.2 | async-start | bytes 3145728 | tf_op jit(solution)/shard_map/all_to_all | solution.py:119
  68.9 12.5 %scatter_fusion.1 = f32[384,2,128]{2,1,0:T(2,128)} fusion(f32[384,2,128]{2,1,0:T(2,128)} %broadcast_in_dim.342, s32[128]{0:T(128)S(1)} %fusion.90, f32[128,2,128]{2,1,0:T(2,128)S(1)} %bitcast.205), kind=kCustom, calls=%fused_computation.5 | custom fusion | bytes 393728 | tf_op jit(solution)/shard_map/scatter | solution.py:19
  81.3 23.5 %all-to-all-done.2 = bf16[32,12,16,128]{3,2,1,0:T(8,128)(2,1)S(1)} async-done(((bf16[32,12,16,128]{3,2,1,0:T(8,128)(2,1)}), bf16[32,12,16,128]{3,2,1,0:T(8,128)(2,1)S(1)}, u32[]{:S(2)}, u32[]{:S(2)}) %all-to-all-start.2) | async-done | bytes 1572896 | tf_op jit(solution)/shard_map/all_to_all | solution.py:119
  104.8 7.4 %all-to-all-start.3 = ((f32[32,12,2,128]{3,2,1,0:T(2,128)}), f32[32,12,2,128]{3,2,1,0:T(2,128)S(1)}, u32[]{:S(2)}, u32[]{:S(2)}) async-start(f32[32,12,2,128]{3,2,1,0:T(2,128)} %bitcast.17), calls=%async_computation.3 | async-start | bytes 786432 | tf_op jit(solution)/shard_map/all_to_all | solution.py:114
  114.5 8.3 %all-to-all-done.3 = f32[32,12,2,128]{3,2,1,0:T(2,128)S(1)} async-done(((f32[32,12,2,128]{3,2,1,0:T(2,128)}), f32[32,12,2,128]{3,2,1,0:T(2,128)S(1)}, u32[]{:S(2)}, u32[]{:S(2)}) %all-to-all-start.3) | async-done | bytes 393248 | tf_op jit(solution)/shard_map/all_to_all | solution.py:114
  122.8 412.1 %while.15 = (s32[]{:T(128)}, f32[2,128,256]{2,1,0:T(8,128)}, f32[6,64,2,128]{3,2,1,0:T(2,128)}, s32[6,64]{1,0:T(8,128)S(1)}, s32[6,64,128]{2,1,0:T(8,128)S(1)}, ...) while((s32[]{:T(128)}, f32[2,128,256]{2,1,0:T(8,128)}, ...), condition=%wide.region_9.10_spmd.clone, body=%wide.region_6.9_spmd.clone.sunk | while | flops 1770383104 | bytes 53107524 | solution.py:68
  122.9 1.0 constant_dynamic-slice_fusion.6
  124.0 2.7 gather_fusion
  126.7 17.1 %fusion.109 = f32[64,128,256]{2,1,0:T(8,128)S(1)} fusion(bf16[64,128,256]{2,1,0:T(8,128)(2,1)} %gather_fusion, pred[64]{0:T(512)(128)(4,1)S(1)} %get-tuple-element.306, s32[64,128]{1,0:T(8,128)S(1)} %add_select_fusion.5, bf16[64,128]{1,0:T(8,128)(2,1)S(1)} %get-tuple-element.309, bf16[64,128]{1,0:T(8,128)(2,1)S(1)} %get-tuple-element.310, ...), kind=kOutput, calls=%fused_computation.27.clone.1 | convolution fusion | flops 573571072 | bytes 12746816 | tf_op jit(solution)/shard_map/while/body/eval_jaxpr/gri,gij->grj/dot_general | solution.py:45
  143.9 13.7 %fusion.110 = (f32[64,128]{1,0:T(8,128)S(1)}, f32[64,128]{1,0:T(8,128)S(1)}) fusion(f32[64,128,256]{2,1,0:T(8,128)S(1)} %fusion.109, bf16[64,128]{1,0:T(8,128)(2,1)S(1)} %get-tuple-element.318, bf16[64,128]{1,0:T(8,128)(2,1)S(1)} %get-tuple-element.319, bf16[64,128]{1,0:T(8,128)(2,1)S(1)} %get-tuple-element.320, ...), kind=kLoop, calls=%fused_computation.10.clone.1 | loop fusion | flops 38780928 | bytes 8617984 | tf_op jit(solution)/shard_map/while/body/eval_jaxpr/reduce_sum | solution.py:48
  158.3 14.2 %fusion.111 = (bf16[64,128,128]{2,1,0:T(8,128)(2,1)}, bf16[64,128,128]{2,1,0:T(8,128)(2,1)}) fusion(f32[64,128]{1,0:T(8,128)S(1)} %get-tuple-element.329, bf16[64,128]{1,0:T(8,128)(2,1)S(1)} %get-tuple-element.318, bf16[64,128]{1,0:T(8,128)(2,1)S(1)} %get-tuple-element.319, bf16[64,128]{1,0:T(8,128)(2,1)S(1)} %get-tuple-element.320, ...), kind=kLoop, calls=%fused_computation.12.clone.1 | loop fusion | flops 38797312 | bytes 4423680 | tf_op jit(solution)/shard_map/convert
  172.5 11.2 %fusion.112 = bf16[64,128,128]{2,1,0:T(8,128)(2,1)S(1)} fusion(s32[64,128]{1,0:T(8,128)S(1)} %add_select_fusion.5, bf16[64,128]{1,0:T(8,128)(2,1)S(1)} %get-tuple-element.309, bf16[64,128]{1,0:T(8,128)(2,1)S(1)} %get-tuple-element.310, bf16[64,128]{1,0:T(8,128)(2,1)S(1)} %get-tuple-element.311, bf16[64,128]{1,0:T(8,128)(2,1)S(1)} %get-tuple-element.312, ...), kind=kLoop, calls=%fused_computation.64.clone.2 | loop fusion | flops 34603008 | bytes 2260992 | tf_op jit(solution)/shard_map/while/body/eval_jaxpr/add | solution.py:27
  183.7 2.9 copy.53
  186.6 4.9 fusion.113
  191.6 1.0 constant_dynamic-slice_fusion.6
  192.7 2.7 gather_fusion
  195.4 17.1 %fusion.109 = f32[64,128,256]{2,1,0:T(8,128)S(1)} fusion(bf16[64,128,256]{2,1,0:T(8,128)(2,1)} %gather_fusion, pred[64]{0:T(512)(128)(4,1)S(1)} %get-tuple-element.306, s32[64,128]{1,0:T(8,128)S(1)} %add_select_fusion.5, bf16[64,128]{1,0:T(8,128)(2,1)S(1)} %get-tuple-element.309, bf16[64,128]{1,0:T(8,128)(2,1)S(1)} %get-tuple-element.310, ...), kind=kOutput, calls=%fused_computation.27.clone.1 | convolution fusion | flops 573571072 | bytes 12746816 | tf_op jit(solution)/shard_map/while/body/eval_jaxpr/gri,gij->grj/dot_general | solution.py:45
  212.6 13.7 %fusion.110 = (f32[64,128]{1,0:T(8,128)S(1)}, f32[64,128]{1,0:T(8,128)S(1)}) fusion(f32[64,128,256]{2,1,0:T(8,128)S(1)} %fusion.109, bf16[64,128]{1,0:T(8,128)(2,1)S(1)} %get-tuple-element.318, bf16[64,128]{1,0:T(8,128)(2,1)S(1)} %get-tuple-element.319, bf16[64,128]{1,0:T(8,128)(2,1)S(1)} %get-tuple-element.320, ...), kind=kLoop, calls=%fused_computation.10.clone.1 | loop fusion | flops 38780928 | bytes 8617984 | tf_op jit(solution)/shard_map/while/body/eval_jaxpr/reduce_sum | solution.py:48
  227.0 14.2 %fusion.111 = (bf16[64,128,128]{2,1,0:T(8,128)(2,1)}, bf16[64,128,128]{2,1,0:T(8,128)(2,1)}) fusion(f32[64,128]{1,0:T(8,128)S(1)} %get-tuple-element.329, bf16[64,128]{1,0:T(8,128)(2,1)S(1)} %get-tuple-element.318, bf16[64,128]{1,0:T(8,128)(2,1)S(1)} %get-tuple-element.319, bf16[64,128]{1,0:T(8,128)(2,1)S(1)} %get-tuple-element.320, ...), kind=kLoop, calls=%fused_computation.12.clone.1 | loop fusion | flops 38797312 | bytes 4423680 | tf_op jit(solution)/shard_map/convert
  241.2 11.2 %fusion.112 = bf16[64,128,128]{2,1,0:T(8,128)(2,1)S(1)} fusion(s32[64,128]{1,0:T(8,128)S(1)} %add_select_fusion.5, bf16[64,128]{1,0:T(8,128)(2,1)S(1)} %get-tuple-element.309, bf16[64,128]{1,0:T(8,128)(2,1)S(1)} %get-tuple-element.310, bf16[64,128]{1,0:T(8,128)(2,1)S(1)} %get-tuple-element.311, bf16[64,128]{1,0:T(8,128)(2,1)S(1)} %get-tuple-element.312, ...), kind=kLoop, calls=%fused_computation.64.clone.2 | loop fusion | flops 34603008 | bytes 2260992 | tf_op jit(solution)/shard_map/while/body/eval_jaxpr/add | solution.py:27
  252.4 2.9 copy.53
  255.3 4.9 fusion.113
  261.3 2.7 gather_fusion
  264.1 17.1 %fusion.109 = f32[64,128,256]{2,1,0:T(8,128)S(1)} fusion(bf16[64,128,256]{2,1,0:T(8,128)(2,1)} %gather_fusion, pred[64]{0:T(512)(128)(4,1)S(1)} %get-tuple-element.306, s32[64,128]{1,0:T(8,128)S(1)} %add_select_fusion.5, bf16[64,128]{1,0:T(8,128)(2,1)S(1)} %get-tuple-element.309, bf16[64,128]{1,0:T(8,128)(2,1)S(1)} %get-tuple-element.310, ...), kind=kOutput, calls=%fused_computation.27.clone.1 | convolution fusion | flops 573571072 | bytes 12746816 | tf_op jit(solution)/shard_map/while/body/eval_jaxpr/gri,gij->grj/dot_general | solution.py:45
  281.2 13.7 %fusion.110 = (f32[64,128]{1,0:T(8,128)S(1)}, f32[64,128]{1,0:T(8,128)S(1)}) fusion(f32[64,128,256]{2,1,0:T(8,128)S(1)} %fusion.109, bf16[64,128]{1,0:T(8,128)(2,1)S(1)} %get-tuple-element.318, bf16[64,128]{1,0:T(8,128)(2,1)S(1)} %get-tuple-element.319, bf16[64,128]{1,0:T(8,128)(2,1)S(1)} %get-tuple-element.320, ...), kind=kLoop, calls=%fused_computation.10.clone.1 | loop fusion | flops 38780928 | bytes 8617984 | tf_op jit(solution)/shard_map/while/body/eval_jaxpr/reduce_sum | solution.py:48
  295.7 14.2 %fusion.111 = (bf16[64,128,128]{2,1,0:T(8,128)(2,1)}, bf16[64,128,128]{2,1,0:T(8,128)(2,1)}) fusion(f32[64,128]{1,0:T(8,128)S(1)} %get-tuple-element.329, bf16[64,128]{1,0:T(8,128)(2,1)S(1)} %get-tuple-element.318, bf16[64,128]{1,0:T(8,128)(2,1)S(1)} %get-tuple-element.319, bf16[64,128]{1,0:T(8,128)(2,1)S(1)} %get-tuple-element.320, ...), kind=kLoop, calls=%fused_computation.12.clone.1 | loop fusion | flops 38797312 | bytes 4423680 | tf_op jit(solution)/shard_map/convert
  309.9 11.2 %fusion.112 = bf16[64,128,128]{2,1,0:T(8,128)(2,1)S(1)} fusion(s32[64,128]{1,0:T(8,128)S(1)} %add_select_fusion.5, bf16[64,128]{1,0:T(8,128)(2,1)S(1)} %get-tuple-element.309, bf16[64,128]{1,0:T(8,128)(2,1)S(1)} %get-tuple-element.310, bf16[64,128]{1,0:T(8,128)(2,1)S(1)} %get-tuple-element.311, bf16[64,128]{1,0:T(8,128)(2,1)S(1)} %get-tuple-element.312, ...), kind=kLoop, calls=%fused_computation.64.clone.2 | loop fusion | flops 34603008 | bytes 2260992 | tf_op jit(solution)/shard_map/while/body/eval_jaxpr/add | solution.py:27
  321.1 2.9 copy.53
  324.0 4.9 fusion.113
  330.0 2.7 gather_fusion
  332.8 17.1 %fusion.109 = f32[64,128,256]{2,1,0:T(8,128)S(1)} fusion(bf16[64,128,256]{2,1,0:T(8,128)(2,1)} %gather_fusion, pred[64]{0:T(512)(128)(4,1)S(1)} %get-tuple-element.306, s32[64,128]{1,0:T(8,128)S(1)} %add_select_fusion.5, bf16[64,128]{1,0:T(8,128)(2,1)S(1)} %get-tuple-element.309, bf16[64,128]{1,0:T(8,128)(2,1)S(1)} %get-tuple-element.310, ...), kind=kOutput, calls=%fused_computation.27.clone.1 | convolution fusion | flops 573571072 | bytes 12746816 | tf_op jit(solution)/shard_map/while/body/eval_jaxpr/gri,gij->grj/dot_general | solution.py:45
  349.9 13.7 %fusion.110 = (f32[64,128]{1,0:T(8,128)S(1)}, f32[64,128]{1,0:T(8,128)S(1)}) fusion(f32[64,128,256]{2,1,0:T(8,128)S(1)} %fusion.109, bf16[64,128]{1,0:T(8,128)(2,1)S(1)} %get-tuple-element.318, bf16[64,128]{1,0:T(8,128)(2,1)S(1)} %get-tuple-element.319, bf16[64,128]{1,0:T(8,128)(2,1)S(1)} %get-tuple-element.320, ...), kind=kLoop, calls=%fused_computation.10.clone.1 | loop fusion | flops 38780928 | bytes 8617984 | tf_op jit(solution)/shard_map/while/body/eval_jaxpr/reduce_sum | solution.py:48
  364.4 14.2 %fusion.111 = (bf16[64,128,128]{2,1,0:T(8,128)(2,1)}, bf16[64,128,128]{2,1,0:T(8,128)(2,1)}) fusion(f32[64,128]{1,0:T(8,128)S(1)} %get-tuple-element.329, bf16[64,128]{1,0:T(8,128)(2,1)S(1)} %get-tuple-element.318, bf16[64,128]{1,0:T(8,128)(2,1)S(1)} %get-tuple-element.319, bf16[64,128]{1,0:T(8,128)(2,1)S(1)} %get-tuple-element.320, ...), kind=kLoop, calls=%fused_computation.12.clone.1 | loop fusion | flops 38797312 | bytes 4423680 | tf_op jit(solution)/shard_map/convert
  378.6 11.2 %fusion.112 = bf16[64,128,128]{2,1,0:T(8,128)(2,1)S(1)} fusion(s32[64,128]{1,0:T(8,128)S(1)} %add_select_fusion.5, bf16[64,128]{1,0:T(8,128)(2,1)S(1)} %get-tuple-element.309, bf16[64,128]{1,0:T(8,128)(2,1)S(1)} %get-tuple-element.310, bf16[64,128]{1,0:T(8,128)(2,1)S(1)} %get-tuple-element.311, bf16[64,128]{1,0:T(8,128)(2,1)S(1)} %get-tuple-element.312, ...), kind=kLoop, calls=%fused_computation.64.clone.2 | loop fusion | flops 34603008 | bytes 2260992 | tf_op jit(solution)/shard_map/while/body/eval_jaxpr/add | solution.py:27
  389.7 2.9 copy.53
  392.6 4.9 fusion.113
  398.7 2.7 gather_fusion
  401.5 17.1 %fusion.109 = f32[64,128,256]{2,1,0:T(8,128)S(1)} fusion(bf16[64,128,256]{2,1,0:T(8,128)(2,1)} %gather_fusion, pred[64]{0:T(512)(128)(4,1)S(1)} %get-tuple-element.306, s32[64,128]{1,0:T(8,128)S(1)} %add_select_fusion.5, bf16[64,128]{1,0:T(8,128)(2,1)S(1)} %get-tuple-element.309, bf16[64,128]{1,0:T(8,128)(2,1)S(1)} %get-tuple-element.310, ...), kind=kOutput, calls=%fused_computation.27.clone.1 | convolution fusion | flops 573571072 | bytes 12746816 | tf_op jit(solution)/shard_map/while/body/eval_jaxpr/gri,gij->grj/dot_general | solution.py:45
  418.6 13.7 %fusion.110 = (f32[64,128]{1,0:T(8,128)S(1)}, f32[64,128]{1,0:T(8,128)S(1)}) fusion(f32[64,128,256]{2,1,0:T(8,128)S(1)} %fusion.109, bf16[64,128]{1,0:T(8,128)(2,1)S(1)} %get-tuple-element.318, bf16[64,128]{1,0:T(8,128)(2,1)S(1)} %get-tuple-element.319, bf16[64,128]{1,0:T(8,128)(2,1)S(1)} %get-tuple-element.320, ...), kind=kLoop, calls=%fused_computation.10.clone.1 | loop fusion | flops 38780928 | bytes 8617984 | tf_op jit(solution)/shard_map/while/body/eval_jaxpr/reduce_sum | solution.py:48
  433.1 14.2 %fusion.111 = (bf16[64,128,128]{2,1,0:T(8,128)(2,1)}, bf16[64,128,128]{2,1,0:T(8,128)(2,1)}) fusion(f32[64,128]{1,0:T(8,128)S(1)} %get-tuple-element.329, bf16[64,128]{1,0:T(8,128)(2,1)S(1)} %get-tuple-element.318, bf16[64,128]{1,0:T(8,128)(2,1)S(1)} %get-tuple-element.319, bf16[64,128]{1,0:T(8,128)(2,1)S(1)} %get-tuple-element.320, ...), kind=kLoop, calls=%fused_computation.12.clone.1 | loop fusion | flops 38797312 | bytes 4423680 | tf_op jit(solution)/shard_map/convert
  447.3 11.2 %fusion.112 = bf16[64,128,128]{2,1,0:T(8,128)(2,1)S(1)} fusion(s32[64,128]{1,0:T(8,128)S(1)} %add_select_fusion.5, bf16[64,128]{1,0:T(8,128)(2,1)S(1)} %get-tuple-element.309, bf16[64,128]{1,0:T(8,128)(2,1)S(1)} %get-tuple-element.310, bf16[64,128]{1,0:T(8,128)(2,1)S(1)} %get-tuple-element.311, bf16[64,128]{1,0:T(8,128)(2,1)S(1)} %get-tuple-element.312, ...), kind=kLoop, calls=%fused_computation.64.clone.2 | loop fusion | flops 34603008 | bytes 2260992 | tf_op jit(solution)/shard_map/while/body/eval_jaxpr/add | solution.py:27
  458.4 2.9 copy.53
  461.3 4.9 fusion.113
  467.4 2.7 gather_fusion
  470.2 17.1 %fusion.109 = f32[64,128,256]{2,1,0:T(8,128)S(1)} fusion(bf16[64,128,256]{2,1,0:T(8,128)(2,1)} %gather_fusion, pred[64]{0:T(512)(128)(4,1)S(1)} %get-tuple-element.306, s32[64,128]{1,0:T(8,128)S(1)} %add_select_fusion.5, bf16[64,128]{1,0:T(8,128)(2,1)S(1)} %get-tuple-element.309, bf16[64,128]{1,0:T(8,128)(2,1)S(1)} %get-tuple-element.310, ...), kind=kOutput, calls=%fused_computation.27.clone.1 | convolution fusion | flops 573571072 | bytes 12746816 | tf_op jit(solution)/shard_map/while/body/eval_jaxpr/gri,gij->grj/dot_general | solution.py:45
  487.3 13.7 %fusion.110 = (f32[64,128]{1,0:T(8,128)S(1)}, f32[64,128]{1,0:T(8,128)S(1)}) fusion(f32[64,128,256]{2,1,0:T(8,128)S(1)} %fusion.109, bf16[64,128]{1,0:T(8,128)(2,1)S(1)} %get-tuple-element.318, bf16[64,128]{1,0:T(8,128)(2,1)S(1)} %get-tuple-element.319, bf16[64,128]{1,0:T(8,128)(2,1)S(1)} %get-tuple-element.320, ...), kind=kLoop, calls=%fused_computation.10.clone.1 | loop fusion | flops 38780928 | bytes 8617984 | tf_op jit(solution)/shard_map/while/body/eval_jaxpr/reduce_sum | solution.py:48
  501.8 14.2 %fusion.111 = (bf16[64,128,128]{2,1,0:T(8,128)(2,1)}, bf16[64,128,128]{2,1,0:T(8,128)(2,1)}) fusion(f32[64,128]{1,0:T(8,128)S(1)} %get-tuple-element.329, bf16[64,128]{1,0:T(8,128)(2,1)S(1)} %get-tuple-element.318, bf16[64,128]{1,0:T(8,128)(2,1)S(1)} %get-tuple-element.319, bf16[64,128]{1,0:T(8,128)(2,1)S(1)} %get-tuple-element.320, ...), kind=kLoop, calls=%fused_computation.12.clone.1 | loop fusion | flops 38797312 | bytes 4423680 | tf_op jit(solution)/shard_map/convert
  515.9 11.2 %fusion.112 = bf16[64,128,128]{2,1,0:T(8,128)(2,1)S(1)} fusion(s32[64,128]{1,0:T(8,128)S(1)} %add_select_fusion.5, bf16[64,128]{1,0:T(8,128)(2,1)S(1)} %get-tuple-element.309, bf16[64,128]{1,0:T(8,128)(2,1)S(1)} %get-tuple-element.310, bf16[64,128]{1,0:T(8,128)(2,1)S(1)} %get-tuple-element.311, bf16[64,128]{1,0:T(8,128)(2,1)S(1)} %get-tuple-element.312, ...), kind=kLoop, calls=%fused_computation.64.clone.2 | loop fusion | flops 34603008 | bytes 2260992 | tf_op jit(solution)/shard_map/while/body/eval_jaxpr/add | solution.py:27
  527.1 2.9 copy.53
  530.0 4.9 fusion.113
  534.9 1.6 convert_element_type.38
  536.6 7.3 %all-to-all-start.4 = ((f32[32,12,2,128]{3,2,1,0:T(2,128)}), f32[32,12,2,128]{3,2,1,0:T(2,128)S(1)}, u32[]{:S(2)}, u32[]{:S(2)}) async-start(f32[32,12,2,128]{3,2,1,0:T(2,128)} %bitcast.199), calls=%async_computation.4 | async-start | bytes 786432 | tf_op jit(solution)/shard_map/all_to_all | solution.py:128
  543.9 10.2 %all-to-all-done.4 = f32[32,12,2,128]{3,2,1,0:T(2,128)S(1)} async-done(((f32[32,12,2,128]{3,2,1,0:T(2,128)}), f32[32,12,2,128]{3,2,1,0:T(2,128)S(1)}, u32[]{:S(2)}, u32[]{:S(2)}) %all-to-all-start.4) | async-done | bytes 393248 | tf_op jit(solution)/shard_map/all_to_all | solution.py:128
  555.7 8.0 %all-gather.3.cloned.1.call-done = bf16[16,128,256]{2,1,0:T(8,128)(2,1)} async-done(((bf16[2,128,256]{2,1,0:T(8,128)(2,1)}), bf16[16,128,256]{2,1,0:T(8,128)(2,1)}) %all-gather.3.cloned.1.call-update) | async-done | bytes 1048592 | tf_op jit(solution)/shard_map/all_gather | solution.py:137
  563.7 2.2 fusion.80
  (154 shorter events, 20.9 us)
Async XLA Ops:
  7.2 536.7 %copy-start = (f32[8,8]{1,0:T(8,128)S(1)}, f32[8,8]{1,0:T(8,128)}, u32[]{:S(2)}) copy-start(f32[8,8]{1,0:T(8,128)} %param.17) | copy-start | bytes 772
  10.7 20.6 %all-to-all-start = ((s32[32,1,12]{2,1,0:T(1,128)}), s32[32,1,12]{2,1,0:T(1,128)S(1)}, u32[]{:S(2)}, u32[]{:S(2)}) async-start(s32[32,1,12]{2,1,0:T(1,128)} %bitcast.4), calls=%async_computation | async-start | bytes 32768 | tf_op jit(solution)/shard_map/all_to_all | solution.py:116
  31.3 27.4 %all-to-all-start.1 = ((s32[32,12,128]{2,1,0:T(8,128)}), s32[32,12,128]{2,1,0:T(8,128)S(1)}, u32[]{:S(2)}, u32[]{:S(2)}) async-start(s32[32,12,128]{2,1,0:T(8,128)} %reshape.378), calls=%async_computation.1 | async-start | bytes 524288 | tf_op jit(solution)/shard_map/all_to_all | solution.py:115
  44.8 24.1 %copy-start.4 = (f32[1,128,2,128]{3,2,1,0:T(2,128)S(1)}, f32[1,128,2,128]{3,2,1,0:T(2,128)}, u32[]{:S(2)}) copy-start(f32[1,128,2,128]{3,2,1,0:T(2,128)} %param.10) | copy-start | bytes 393220
  58.7 64.2 %copy-start.1 = (bf16[1,2,128,256]{3,2,1,0:T(8,128)(2,1)S(1)}, bf16[1,2,128,256]{3,2,1,0:T(8,128)(2,1)}, u32[]{:S(2)}) copy-start(bf16[1,2,128,256]{3,2,1,0:T(8,128)(2,1)} %param.15) | copy-start | bytes 393220
  58.7 46.1 %all-to-all-start.2 = ((bf16[32,12,16,128]{3,2,1,0:T(8,128)(2,1)}), bf16[32,12,16,128]{3,2,1,0:T(8,128)(2,1)S(1)}, u32[]{:S(2)}, u32[]{:S(2)}) async-start(bf16[32,12,16,128]{3,2,1,0:T(8,128)(2,1)} %bitcast.13), calls=%async_computation.2 | async-start | bytes 3145728 | tf_op jit(solution)/shard_map/all_to_all | solution.py:119
  104.8 18.0 %all-to-all-start.3 = ((f32[32,12,2,128]{3,2,1,0:T(2,128)}), f32[32,12,2,128]{3,2,1,0:T(2,128)S(1)}, u32[]{:S(2)}, u32[]{:S(2)}) async-start(f32[32,12,2,128]{3,2,1,0:T(2,128)} %bitcast.17), calls=%async_computation.3 | async-start | bytes 786432 | tf_op jit(solution)/shard_map/all_to_all | solution.py:114
  112.2 451.5 %all-gather.3.cloned.1.call-start = ((), (), s32[]{:S(2)}) async-start(), calls=%async_computation.5 | async-start | bytes 1179648 | tf_op jit(solution)/shard_map/all_gather | solution.py:137
  122.8 34.8 %copy-start.2 = (f32[6,64,2,128]{3,2,1,0:T(2,128)}, f32[6,64,2,128]{3,2,1,0:T(2,128)S(1)}, u32[]{:S(2)}) copy-start(f32[6,64,2,128]{3,2,1,0:T(2,128)S(1)} %get-tuple-element.362) | copy-start | bytes 1179652 | tf_op jit(solution)/shard_map/while
  186.6 4.9 copy-start.3
  191.5 34.8 %copy-start.2 = (f32[6,64,2,128]{3,2,1,0:T(2,128)}, f32[6,64,2,128]{3,2,1,0:T(2,128)S(1)}, u32[]{:S(2)}) copy-start(f32[6,64,2,128]{3,2,1,0:T(2,128)S(1)} %get-tuple-element.362) | copy-start | bytes 1179652 | tf_op jit(solution)/shard_map/while
  255.3 4.9 copy-start.3
  260.2 34.8 %copy-start.2 = (f32[6,64,2,128]{3,2,1,0:T(2,128)}, f32[6,64,2,128]{3,2,1,0:T(2,128)S(1)}, u32[]{:S(2)}) copy-start(f32[6,64,2,128]{3,2,1,0:T(2,128)S(1)} %get-tuple-element.362) | copy-start | bytes 1179652 | tf_op jit(solution)/shard_map/while
  324.0 4.9 copy-start.3
  328.9 34.8 %copy-start.2 = (f32[6,64,2,128]{3,2,1,0:T(2,128)}, f32[6,64,2,128]{3,2,1,0:T(2,128)S(1)}, u32[]{:S(2)}) copy-start(f32[6,64,2,128]{3,2,1,0:T(2,128)S(1)} %get-tuple-element.362) | copy-start | bytes 1179652 | tf_op jit(solution)/shard_map/while
  392.6 4.9 copy-start.3
  397.5 34.8 %copy-start.2 = (f32[6,64,2,128]{3,2,1,0:T(2,128)}, f32[6,64,2,128]{3,2,1,0:T(2,128)S(1)}, u32[]{:S(2)}) copy-start(f32[6,64,2,128]{3,2,1,0:T(2,128)S(1)} %get-tuple-element.362) | copy-start | bytes 1179652 | tf_op jit(solution)/shard_map/while
  461.3 4.9 copy-start.3
  466.2 34.8 %copy-start.2 = (f32[6,64,2,128]{3,2,1,0:T(2,128)}, f32[6,64,2,128]{3,2,1,0:T(2,128)S(1)}, u32[]{:S(2)}) copy-start(f32[6,64,2,128]{3,2,1,0:T(2,128)S(1)} %get-tuple-element.362) | copy-start | bytes 1179652 | tf_op jit(solution)/shard_map/while
  530.0 4.9 copy-start.3
  536.6 17.6 %all-to-all-start.4 = ((f32[32,12,2,128]{3,2,1,0:T(2,128)}), f32[32,12,2,128]{3,2,1,0:T(2,128)S(1)}, u32[]{:S(2)}, u32[]{:S(2)}) async-start(f32[32,12,2,128]{3,2,1,0:T(2,128)} %bitcast.199), calls=%async_computation.4 | async-start | bytes 786432 | tf_op jit(solution)/shard_map/all_to_all | solution.py:128
Sparse Core Ops, SparseCore 0:
  536.7 27.0 all-gather.2
where the time goes:
time: 574 us; the launch traced here: 573 us
  other arithmetic  244 us (43%)
  matrix products  139 us (24%)
  local copies, waits for them, and re-layouts  79.3 us (14%)
  waiting for transfers between devices  53 us (9%)
  starting transfers between devices  42.4 us (7%)
  between operations  14.2 us (2%)
    dot_general x6, matrix products, advance(): jnp.einsum('gri,gij->grj', row_matrix, chosen, preferred_element_type=jnp...  103 us
    another operation x6, other arithmetic  85.2 us
    reduce_sum x6, other arithmetic, advance(): model_real = jnp.sum(partial_value[:, :, :side] * column_matrix, axis=2)  82.1 us
    add x6, other arithmetic, spread_taps(): matrix + jnp.where(offset == which, taps[:, which, :, None], jnp.zeros(()...  67 us
    dot_general x6, matrix products, advance(): jnp.einsum('gtri,grj->tij', masked_rows, weighted, preferred_element_type...  29.4 us
    scatter x4, local copies, waits for them, and re-layouts, place_slots(): return empty.at[slot].set(values)  26.7 us
    all_to_all x1, waiting for transfers between devices, body(): lax.all_to_all(sent_taps, 'tile', split_axis=0, concat_axis=0, tiled=True)  23.5 us
    add x6, local copies, waits for them, and re-layouts, spread_taps(): matrix + jnp.where(offset == which, taps[:, which, :, None], jnp.zeros(()...  17.4 us
  transfers between devices with their start and end apart: 6, of which 5 were waited for; matrix products, arithmetic and copies ran while one was open for 8% of the time, Pallas kernels for 0%

commit v1 on v0

v1 whole, which is shorter than its diff:
```python
import functools

import jax
import jax.numpy as jnp
from jax import lax
from jax.experimental import pallas as pl
from jax.experimental.pallas import tpu as pltpu
from jax.sharding import PartitionSpec as P

SHIFT = 65536


def spread(start, table_row, table, lanes):
    sub = lax.broadcasted_iota(jnp.int32, (8, lanes), 0)
    taps = jnp.take_along_axis(table, jnp.broadcast_to(table_row, (8, lanes)), axis=1, mode="promise_in_bounds")
    offset = sub - start
    folded = jnp.take_along_axis(taps, jnp.bitwise_and(offset, 7), axis=0, mode="promise_in_bounds")
    return folded, lax.shift_right_arithmetic(offset, 3)


def twice(folded, group):
    values = jnp.concatenate([folded, folded], axis=0).astype(jnp.bfloat16)
    groups = jnp.concatenate([group, group + 1], axis=0).astype(jnp.float32).astype(jnp.bfloat16)
    return values, groups


def work_chunk(rec, model_t, table, row_ref, weighted_ref, emit, capacity, side):
    lanes = 128
    zero16 = jnp.zeros((16, lanes), jnp.bfloat16)
    column = []
    for k in range(capacity):
        position = rec(k, 2).astype(jnp.int32)
        lookup = rec(k, 3).astype(jnp.int32)
        folded, group = spread(lax.shift_right_logical(position, 16), lax.shift_right_logical(lookup, 16), table, lanes)
        values, groups = twice(folded, group)
        for tile in range(2 * side // 16):
            row_ref[pl.ds(16 * tile, 16), pl.ds(k * lanes, lanes)] = jnp.where(
                groups == jnp.bfloat16(-2 * tile), values, zero16
            )
        column.append(
            spread(jnp.bitwise_and(position, SHIFT - 1), jnp.bitwise_and(lookup, SHIFT - 1), table, lanes)
        )
    for pair in range(capacity // 2):
        partial = jnp.dot(
            model_t, row_ref[:, pl.ds(pair * 2 * lanes, 2 * lanes)], preferred_element_type=jnp.float32
        )
        for half in range(2):
            k = 2 * pair + half
            folded, group = column[k]
            block = partial[:, half * lanes : (half + 1) * lanes]
            picked = [jnp.zeros((8, lanes), jnp.float32)] * 2
            for tile in range(side // 8):
                hit = group == -tile
                for part in range(2):
                    start = part * side + 8 * tile
                    picked[part] = jnp.where(hit, block[start : start + 8], picked[part])
            for part in range(2):
                residual = rec(k, part) - jnp.sum(picked[part] * folded, axis=0, keepdims=True)
                emit(k, part, residual)
                values, groups = twice(residual * folded, group)
                for tile in range(side // 16):
                    weighted_ref[pl.ds(part * side + 16 * tile, 16), pl.ds(k * lanes, lanes)] = jnp.where(
                        groups == jnp.bfloat16(-2 * tile), values, zero16
                    )


def compute_kernel(capacity, side, rec_ref, model_ref, table_ref, residual_ref, grid_ref, row_ref, weighted_ref, total_ref):
    step = pl.program_id(0)

    @pl.when(step == 0)
    def _():
        total_ref[...] = jnp.zeros_like(total_ref)

    def rec(k, which):
        return rec_ref[0, k, pl.ds(which, 1), :]

    def emit(k, part, value):
        residual_ref[0, k, pl.ds(part, 1), :] = value

    work_chunk(rec, model_ref[...], table_ref[...], row_ref, weighted_ref, emit, capacity, side)
    total_ref[...] += lax.dot_general(
        row_ref[...], weighted_ref[...], (((1,), (1,)), ((), ())), preferred_element_type=jnp.float32
    )

    @pl.when(step == pl.num_programs(0) - 1)
    def _():
        grid_ref[...] = total_ref[...].astype(jnp.bfloat16)


def degrid_grid(records, model, table):
    owners, capacity = records.shape[:2]
    tiles, side = model.shape[0], model.shape[1]
    model_t = model.reshape(tiles * side, 2 * side).T
    return pl.pallas_call(
        functools.partial(compute_kernel, capacity, side),
        grid=(owners,),
        out_shape=(
            jax.ShapeDtypeStruct((owners, capacity, 2, 128), jnp.float32),
            jax.ShapeDtypeStruct((tiles * side, 2 * side), jnp.bfloat16),
        ),
        in_specs=[
            pl.BlockSpec((1, capacity, 4, 128), lambda i: (i, 0, 0, 0)),
            pl.BlockSpec((2 * side, tiles * side), lambda i: (0, 0)),
            pl.BlockSpec((8, 128), lambda i: (0, 0)),
        ],
        out_specs=[
            pl.BlockSpec((1, capacity, 2, 128), lambda i: (i, 0, 0, 0)),
            pl.BlockSpec((tiles * side, 2 * side), lambda i: (0, 0)),
        ],
        scratch_shapes=[
            pltpu.VMEM((tiles * side, capacity * 128), jnp.bfloat16),
            pltpu.VMEM((2 * side, capacity * 128), jnp.bfloat16),
            pltpu.VMEM((tiles * side, 2 * side), jnp.float32),
        ],
        compiler_params=pltpu.CompilerParams(vmem_limit_bytes=32 << 20),
    )(records, model_t, table)


def body(visibilities, uv_cell, sub_pixel, w_plane, block_tile, model_grid, kernel_table, coupling):
    blocks = visibilities.shape[1]
    rows = visibilities.shape[3]
    owners = lax.axis_size("tile")
    capacity = 3 * blocks // owners
    total = owners * capacity
    tiles_here = model_grid.shape[1]
    side = model_grid.shape[2]
    oversample = kernel_table.shape[1]
    support = kernel_table.shape[2]
    tile_id = block_tile[0]
    owner = tile_id // tiles_here
    local_tile = tile_id % tiles_here
    order = jnp.arange(blocks, dtype=jnp.int32)
    same = (owner[:, None] == owner[None, :]) & (order[None, :] < order[:, None])
    slot = owner * capacity + jnp.sum(same.astype(jnp.int32), axis=1)
    holds = slot[None, :] == jnp.arange(total, dtype=jnp.int32)[:, None]
    source = jnp.sum(jnp.where(holds, order[None, :], 0), axis=1)
    filled = jnp.any(holds, axis=1)
    cells = uv_cell[0]
    lookup = w_plane[0][:, None, None] * oversample + sub_pixel[0]
    position = (cells[:, 0] + side * local_tile[:, None]) * SHIFT + cells[:, 1]
    records = jnp.concatenate(
        [
            visibilities[0],
            position[:, None].astype(jnp.float32),
            (lookup[:, 0] * SHIFT + lookup[:, 1])[:, None].astype(jnp.float32),
        ],
        axis=1,
    )
    empty = jnp.array([0.0, 0.0, tiles_here * side * SHIFT, 0.0], jnp.float32)[None, :, None]
    sent = jnp.where(filled[:, None, None], jnp.take(records, source, axis=0), empty)
    got = lax.all_to_all(sent.reshape(owners, capacity, 4, rows), "tile", split_axis=0, concat_axis=0, tiled=True)
    table = kernel_table.reshape(-1, support).T.astype(jnp.float32)
    residual, grid_rounded = degrid_grid(got, model_grid[0], table)
    returned = lax.all_to_all(residual, "tile", split_axis=0, concat_axis=0, tiled=True)
    residuals = jnp.take(returned.reshape(total, 2, rows), slot, axis=0)[None]
    grid_rounded = grid_rounded.reshape(1, tiles_here, side, 2 * side)
    own_row = lax.dynamic_index_in_dim(coupling, lax.axis_index("freq"), 0, keepdims=False)
    coupled_grid = jnp.sum(
        own_row[:, None, None, None]
        * lax.all_gather(grid_rounded, "freq", axis=0, tiled=True).astype(jnp.float32),
        axis=0,
    )[None]
    return (residuals, coupled_grid)


def solution(mesh):
    return jax.shard_map(
        body,
        mesh=mesh,
        in_specs=(
            P("freq", "tile", None, None),
            P("freq", "tile", None, None),
            P("freq", "tile", None, None),
            P("freq", "tile"),
            P("freq", "tile"),
            P("freq", "tile", None, None),
            P(),
            P(),
        ),
        out_specs=(P("freq", "tile", None, None), P("freq", "tile", None, None)),
        check_vma=False,
    )
```

time: 574 us -> 116 us (0.20)
  other arithmetic: 244 us -> 9.78 us
  matrix products: 139 us -> 0 us
  local copies, waits for them, and re-layouts: 79.3 us -> 4.21 us
  Pallas kernels: 0 us -> 30.8 us
  starting transfers between devices: 42.4 us -> 20.6 us
  waiting for transfers between devices: 53 us -> 35.9 us
    dot_general x14 -> x0, matrix products: 139 us -> none  [the longest x6 103 us: advance(): jnp.einsum('gri,gij->grj', row_matrix, chosen, preferred_element_type=jnp...]
    another operation x7 -> x0, other arithmetic: 85.3 us -> none
    reduce_sum x7 -> x2, other arithmetic: 82.3 us -> 0.32 us  [the longest x1 0.17 us: body(): slot = owner * capacity + jnp.sum(same.astype(jnp.int32), axis=1)]
    add x8 -> x1, other arithmetic: 68.1 us -> 0.98 us  [body(): lookup = w_plane[0][:, None, None] * oversample + sub_pixel[0]]
    pallas_call x0 -> x1, Pallas kernels: none -> 30.8 us  [degrid_grid(): pl.pallas_call(functools.partial(compute_kernel, capacity, side), grid=(o...]
    scatter x4 -> x0, local copies, waits for them, and re-layouts: 26.7 us -> none  [place_slots(): return empty.at[slot].set(values)]
    all_to_all x5 -> x2, starting transfers between devices: 42.3 us -> 20.5 us  [the longest x1 12.2 us: body(): lax.all_to_all(sent.reshape(owners, capacity, 4, rows), 'tile', split_axi...]
    add x6 -> x0, local copies, waits for them, and re-layouts: 17.4 us -> none  [spread_taps(): matrix + jnp.where(offset == which, taps[:, which, :, None], jnp.zeros(()...]
  transfers between devices with their start and end apart: 6 -> 3, of which waited for: 5 -> 3; matrix products, arithmetic and copies ran while one was open for 8% -> 2% of each run, Pallas kernels for 0% -> 0%
where the time goes in v1:
time: 116 us; the launch traced here: 115 us
  waiting for transfers between devices  35.9 us (31%)
  Pallas kernels  30.8 us (27%)
  starting transfers between devices  20.6 us (18%)
  between operations  14.2 us (12%)
  other arithmetic  9.78 us (8%)
  local copies, waits for them, and re-layouts  4.21 us (4%)
    pallas_call x1, Pallas kernels, degrid_grid(): pl.pallas_call(functools.partial(compute_kernel, capacity, side), grid=(o...  30.8 us
    all_to_all x1, waiting for transfers between devices, body(): lax.all_to_all(sent.reshape(owners, capacity, 4, rows), 'tile', split_axi...  18.9 us
    all_to_all x1, starting transfers between devices, body(): lax.all_to_all(sent.reshape(owners, capacity, 4, rows), 'tile', split_axi...  12.2 us
    all_to_all x1, waiting for transfers between devices, body(): lax.all_to_all(residual, 'tile', split_axis=0, concat_axis=0, tiled=True)  10.7 us
    all_to_all x1, starting transfers between devices, body(): lax.all_to_all(residual, 'tile', split_axis=0, concat_axis=0, tiled=True)  8.37 us
    all_gather x1, waiting for transfers between devices, body(): lax.all_gather(grid_rounded, 'freq', axis=0, tiled=True).astype(jnp.float32)  6.3 us
  transfers between devices with their start and end apart: 3, of which 3 were waited for; matrix products, arithmetic and copies ran while one was open for 2% of the time, Pallas kernels for 0%

profile of v1, /device:TPU:1, one launch (start us, length us, event | category | flops | bytes accessed | tf_op | source)
XLA Modules:
  0.0 115.5 jit_solution(9331135380472610544)
XLA Ops:
  7.2 0.0 copy-start
  7.2 0.0 copy-start.2
  7.2 0.7 and_select_fusion.3
  7.9 0.7 fusion.9
  8.6 0.2 convert_reduce_fusion
  8.7 0.7 fusion.8
  9.4 0.1 select_reduce_fusion
  9.6 0.1 reduce_sum.38
  9.7 0.2 fusion
  9.8 0.9 copy.28
  10.8 0.7 multiply_bitcast_fusion
  11.4 1.0 bitcast_add_fusion
  12.5 0.1 broadcast_in_dim.68
  12.6 0.1 fusion.2
  12.7 0.0 copy-done.2
  12.7 0.0 copy-start.4
  12.7 0.2 pad_maximum_fusion
  12.9 2.0 %gather_fusion = f32[384,4,128]{2,1,0:T(4,128)S(1)} fusion(f32[128,4,128]{2,1,0:T(4,128)S(1)} %pad_maximum_fusion, s32[1024]{0:T(1024)S(1)} %pad_clamp_fusion.1), kind=kCustom, calls=%fused_computation | custom fusion | bytes 1574400 | tf_op jit(solution)/shard_map/jit(_take)/gather | solution.py:150
  14.9 0.0 copy-done.4
  14.9 2.2 %select_select_fusion = f32[32,12,4,128]{3,2,1,0:T(4,128)} fusion(f32[32,12,4,128]{3,2,1,0:T(4,128)S(1)} %bitcast.64, f32[4]{0:T(128)S(1)} %copy-done.4, pred[32,12]{1,0:T(8,128)(4,1)S(1)} %compare_and_fusion, pred[32,12]{1,0:T(8,128)(4,1)S(1)} %broadcast_in_dim.68), kind=kLoop, calls=%fused_computation.3 | loop fusion | flops 393216 | bytes 1573648 | tf_op jit(solution)/shard_map/jit(_where)/select_n | solution.py:150
  17.1 0.0 copy-start.1
  17.1 0.0 copy-start.3
  17.1 12.2 %all-to-all-start = ((f32[32,12,4,128]{3,2,1,0:T(4,128)}), f32[32,12,4,128]{3,2,1,0:T(4,128)S(1)}, u32[]{:S(2)}, u32[]{:S(2)}) async-start(f32[32,12,4,128]{3,2,1,0:T(4,128)} %select_select_fusion), calls=%async_computation | async-start | bytes 1572864 | tf_op jit(solution)/shard_map/all_to_all | solution.py:151
  29.3 0.0 all-gather.2.cloned.1.call-start
  29.3 0.0 copy-done.1
  29.3 0.1 copy.25
  29.4 0.0 copy-done.3
  29.5 0.0 copy-start.5
  29.5 0.1 copy.24
  29.6 0.1 reshape.196
  29.7 18.9 %all-to-all-done.rec_ref = f32[32,12,4,128]{3,2,1,0:T(4,128)S(1)} async-done(((f32[32,12,4,128]{3,2,1,0:T(4,128)}), f32[32,12,4,128]{3,2,1,0:T(4,128)S(1)}, u32[]{:S(2)}, u32[]{:S(2)}) %all-to-all-start) | async-done | bytes 786464 | tf_op jit(solution)/shard_map/all_to_all | solution.py:151
  48.5 30.8 %shard_map.104 = (f32[32,12,2,128]{3,2,1,0:T(2,128)}, bf16[256,256]{1,0:T(8,128)(2,1)}) custom-call(f32[32,12,4,128]{3,2,1,0:T(4,128)S(1)} %all-to-all-done.rec_ref, bf16[256,256]{1,0:T(8,128)(2,1)S(1)} %bitcast.62, f32[8,128]{1,0:T(8,128)S(1)} %bitcast.63), custom_call_target="tpu_custom_call" | custom-call | tf_op jit(solution)/shard_map/pallas_call | solution.py:94
  79.3 0.0 all-gather.2.cloned.1.call-update
  79.3 8.4 %all-to-all-start.1 = ((f32[32,12,2,128]{3,2,1,0:T(2,128)}), f32[32,12,2,128]{3,2,1,0:T(2,128)S(1)}, u32[]{:S(2)}, u32[]{:S(2)}) async-start(f32[32,12,2,128]{3,2,1,0:T(2,128)} %get-tuple-element.4), calls=%async_computation.1 | async-start | bytes 786432 | tf_op jit(solution)/shard_map/all_to_all | solution.py:154
  87.7 0.0 copy-done
  87.8 0.0 copy-done.5
  87.8 10.7 %all-to-all-done.1 = f32[32,12,2,128]{3,2,1,0:T(2,128)S(1)} async-done(((f32[32,12,2,128]{3,2,1,0:T(2,128)}), f32[32,12,2,128]{3,2,1,0:T(2,128)S(1)}, u32[]{:S(2)}, u32[]{:S(2)}) %all-to-all-start.1) | async-done | bytes 393248 | tf_op jit(solution)/shard_map/all_to_all | solution.py:154
  98.5 0.7 gather_fusion.1
  99.3 0.9 bitcast_select_fusion
  100.1 6.3 %all-gather.2.cloned.1.call-done = bf16[8,2,128,256]{3,2,1,0:T(8,128)(2,1)} async-done(((bf16[1,2,128,256]{3,2,1,0:T(8,128)(2,1)}), bf16[8,2,128,256]{3,2,1,0:T(8,128)(2,1)}) %all-gather.2.cloned.1.call-update) | async-done | bytes 1048592 | tf_op jit(solution)/shard_map/all_gather | solution.py:160
  106.4 2.2 %multiply_reduce_fusion = f32[2,128,256]{2,1,0:T(8,128)} fusion(bf16[8,2,128,256]{3,2,1,0:T(8,128)(2,1)} %all-gather.2.cloned.1.call-done, f32[8]{0:T(128)S(1)} %dynamic-slice_bitcast_fusion), kind=kLoop, calls=%fused_computation.2 | loop fusion | flops 1507328 | bytes 1310752 | tf_op jit(solution)/shard_map/reduce_sum | solution.py:158
  (8 shorter events, 0.1 us)
Async XLA Ops:
  7.2 80.6 %copy-start = (f32[8,8]{1,0:T(8,128)S(1)}, f32[8,8]{1,0:T(8,128)}, u32[]{:S(2)}) copy-start(f32[8,8]{1,0:T(8,128)} %param.16) | copy-start | bytes 772
  7.2 5.5 %copy-start.2 = (f32[1,128,2,128]{3,2,1,0:T(2,128)S(1)}, f32[1,128,2,128]{3,2,1,0:T(2,128)}, u32[]{:S(2)}) copy-start(f32[1,128,2,128]{3,2,1,0:T(2,128)} %param.9) | copy-start | bytes 393220
  12.7 2.2 %copy-start.4 = (f32[4]{0:T(128)S(1)}, f32[4]{0:T(128)}, u32[]{:S(2)}) copy-start(f32[4]{0:T(128)} %constant.77.clone) | copy-start | bytes 52
  17.1 12.2 %copy-start.1 = (bf16[1,2,128,256]{3,2,1,0:T(8,128)(2,1)S(1)}, bf16[1,2,128,256]{3,2,1,0:T(8,128)(2,1)}, u32[]{:S(2)}) copy-start(bf16[1,2,128,256]{3,2,1,0:T(8,128)(2,1)} %param.14) | copy-start | bytes 393220
  17.1 12.3 %copy-start.3 = (bf16[16,8,8]{0,2,1:T(8,128)(2,1)S(1)}, bf16[16,8,8]{0,2,1:T(8,128)(2,1)}, u32[]{:S(2)}) copy-start(bf16[16,8,8]{0,2,1:T(8,128)(2,1)} %param.15) | copy-start | bytes 6148
  17.1 31.4 %all-to-all-start = ((f32[32,12,4,128]{3,2,1,0:T(4,128)}), f32[32,12,4,128]{3,2,1,0:T(4,128)S(1)}, u32[]{:S(2)}, u32[]{:S(2)}) async-start(f32[32,12,4,128]{3,2,1,0:T(4,128)} %select_select_fusion), calls=%async_computation | async-start | bytes 1572864 | tf_op jit(solution)/shard_map/all_to_all | solution.py:151
  29.3 77.1 %all-gather.2.cloned.1.call-start = ((), (), s32[]{:S(2)}) async-start(), calls=%async_computation.2 | async-start | bytes 1179648 | tf_op jit(solution)/shard_map/all_gather | solution.py:160
  29.5 58.3 %copy-start.5 = (s32[1,128]{1,0:T(1,128)S(1)}, s32[1,128]{1,0:T(1,128)}, u32[]{:S(2)}) copy-start(s32[1,128]{1,0:T(1,128)} %param.13) | copy-start | bytes 1540
  79.3 19.2 %all-to-all-start.1 = ((f32[32,12,2,128]{3,2,1,0:T(2,128)}), f32[32,12,2,128]{3,2,1,0:T(2,128)S(1)}, u32[]{:S(2)}, u32[]{:S(2)}) async-start(f32[32,12,2,128]{3,2,1,0:T(2,128)} %get-tuple-element.4), calls=%async_computation.1 | async-start | bytes 786432 | tf_op jit(solution)/shard_map/all_to_all | solution.py:154
Sparse Core Ops, SparseCore 0:
  79.5 26.9 all-gather.1

commit v2 on v1

v2 whole, which is shorter than its diff:
```python
import functools

import jax
import jax.numpy as jnp
from jax import lax
from jax.experimental import pallas as pl
from jax.experimental.pallas import tpu as pltpu
from jax.sharding import PartitionSpec as P

SHIFT = 65536


def spread(start, table_row, table, lanes):
    sub = lax.broadcasted_iota(jnp.int32, (8, lanes), 0)
    taps = jnp.take_along_axis(table, jnp.broadcast_to(table_row, (8, lanes)), axis=1, mode="promise_in_bounds")
    offset = sub - start
    folded = jnp.take_along_axis(taps, jnp.bitwise_and(offset, 7), axis=0, mode="promise_in_bounds")
    return folded, lax.shift_right_arithmetic(offset, 3)


def twice(folded, group):
    values = jnp.concatenate([folded, folded], axis=0).astype(jnp.bfloat16)
    groups = jnp.concatenate([group, group + 1], axis=0).astype(jnp.float32).astype(jnp.bfloat16)
    return values, groups


def work_chunk(rec, model_t, table, row_ref, weighted_ref, emit, capacity, side):
    lanes = 128
    zero16 = jnp.zeros((16, lanes), jnp.bfloat16)
    column = []
    for k in range(capacity):
        position = rec(k, 2).astype(jnp.int32)
        lookup = rec(k, 3).astype(jnp.int32)
        folded, group = spread(lax.shift_right_logical(position, 16), lax.shift_right_logical(lookup, 16), table, lanes)
        values, groups = twice(folded, group)
        for tile in range(2 * side // 16):
            row_ref[pl.ds(16 * tile, 16), pl.ds(k * lanes, lanes)] = jnp.where(
                groups == jnp.bfloat16(-2 * tile), values, zero16
            )
        column.append(
            spread(jnp.bitwise_and(position, SHIFT - 1), jnp.bitwise_and(lookup, SHIFT - 1), table, lanes)
        )
    for pair in range(capacity // 2):
        partial = jnp.dot(
            model_t, row_ref[:, pl.ds(pair * 2 * lanes, 2 * lanes)], preferred_element_type=jnp.float32
        )
        for half in range(2):
            k = 2 * pair + half
            folded, group = column[k]
            block = partial[:, half * lanes : (half + 1) * lanes]
            picked = [jnp.zeros((8, lanes), jnp.float32)] * 2
            for tile in range(side // 8):
                hit = group == -tile
                for part in range(2):
                    start = part * side + 8 * tile
                    picked[part] = jnp.where(hit, block[start : start + 8], picked[part])
            for part in range(2):
                residual = rec(k, part) - jnp.sum(picked[part] * folded, axis=0, keepdims=True)
                emit(k, part, residual)
                values, groups = twice(residual * folded, group)
                for tile in range(side // 16):
                    weighted_ref[pl.ds(part * side + 16 * tile, 16), pl.ds(k * lanes, lanes)] = jnp.where(
                        groups == jnp.bfloat16(-2 * tile), values, zero16
                    )


MESH = pl.DeviceIdType.MESH


def kernel(
    dims,
    tile_s, plane_s, coupling_s, tile_v, samples, cells, offsets, model, table_ref,
    residual_out, coupled_out,
    records, index_v, index_s, model_t, send, got, solved, returned,
    row0, row1, weighted0, weighted1, total, grids,
    index_sem, send_sem, got_sem, back_sem, home_sem, grid_send, grid_got,
):
    owners, capacity, tiles, side, oversample, chips_y, chips_x = dims
    chips_z = owners // chips_y
    blocks = samples.shape[0]
    lanes = 128
    me = lax.axis_index("tile")
    plane = lax.axis_index("freq")
    mine_y, mine_z = me // chips_z, lax.rem(me, chips_z)
    mine_x, core = plane // 2, lax.rem(plane, 2)

    def hop(n):
        group, across = n // chips_y, lax.rem(n, chips_y)
        along = (group + 1) // 2 * (2 * lax.rem(group, 2) - 1)
        return across, along

    def target(n):
        across, along = hop(n)
        return lax.rem(mine_y + across, chips_y) * chips_z + lax.rem(mine_z + along + chips_z, chips_z)

    def origin(n):
        across, along = hop(n)
        return lax.rem(mine_y - across + chips_y, chips_y) * chips_z + lax.rem(mine_z - along + chips_z, chips_z)

    sibling = 2 * mine_x + 1 - core
    ahead = 2 * lax.rem(mine_x + 1, chips_x) + core
    behind = 2 * lax.rem(mine_x + chips_x - 1, chips_x) + core
    opposite = 2 * lax.rem(mine_x + 2, chips_x) + core

    barrier = pltpu.get_barrier_semaphore()

    def greet(n, carry):
        pl.semaphore_signal(barrier, inc=1, device_id=(target(n), plane), device_id_type=MESH)
        return carry

    lax.fori_loop(1, owners, greet, 0)
    for other in (sibling, ahead, behind):
        pl.semaphore_signal(barrier, inc=1, device_id=(me, other), device_id_type=MESH)

    owner = lax.shift_right_logical(tile_v[...], tiles.bit_length() - 1)
    wide = (blocks, lanes)
    down = lax.broadcasted_iota(jnp.int32, wide, 0)
    over = lax.broadcasted_iota(jnp.int32, wide, 1)

    def stand(row):
        return jnp.broadcast_to(row.astype(jnp.float32), wide).T.astype(jnp.int32)

    same = (stand(owner) == owner) & (down < over)
    slot = owner * capacity + jnp.sum(same.astype(jnp.int32), axis=0, keepdims=True)
    slots = stand(slot)
    for part in range(owners * capacity // lanes):
        index_v[pl.ds(part, 1), :] = blocks + jnp.sum(
            jnp.where(slots == over + part * lanes, down - blocks, 0), axis=0, keepdims=True
        )
    index_v[pl.ds(owners * capacity // lanes, 1), :] = slot
    index_copy = pltpu.make_async_copy(index_v, index_s, index_sem)
    index_copy.start()

    def fill(b, carry):
        tile = lax.rem(tile_s[0, b], tiles)
        base = plane_s[0, b] * oversample
        records[b, pl.ds(0, 2), :] = samples[b]
        place = (cells[b, pl.ds(0, 1), :] + tile * side) * SHIFT + cells[b, pl.ds(1, 1), :]
        lookup = (offsets[b, pl.ds(0, 1), :] + base) * SHIFT + offsets[b, pl.ds(1, 1), :] + base
        records[b, pl.ds(2, 1), :] = place.astype(jnp.float32)
        records[b, pl.ds(3, 1), :] = lookup.astype(jnp.float32)
        return carry

    lax.fori_loop(0, blocks, fill, 0, unroll=8)
    records[blocks] = jnp.where(
        lax.broadcasted_iota(jnp.int32, (4, lanes), 0) == 2, jnp.float32(tiles * side * SHIFT), jnp.float32(0)
    )
    index_copy.wait()
    pl.semaphore_wait(barrier, owners + 2)

    def outward(n):
        to = target(n)
        return pltpu.make_async_remote_copy(
            src_ref=send.at[to], dst_ref=got.at[me], send_sem=send_sem.at[to], recv_sem=got_sem.at[me],
            device_id=(to, plane), device_id_type=MESH,
        )

    def pack(to):
        for j in range(capacity):
            s = to * capacity + j
            send[to, j] = records[index_s[s // lanes, lax.rem(s, lanes)]]

    def dispatch(n, carry):
        pack(target(n))
        outward(n).start()
        return carry

    lax.fori_loop(1, owners, dispatch, 0)
    pack(me)
    own = pltpu.make_async_copy(send.at[me], got.at[me], got_sem.at[me])
    own.start()
    model_t[...] = model[...].T
    total[...] = jnp.zeros_like(total)
    row1[...] = jnp.zeros_like(row1)
    weighted1[...] = jnp.zeros_like(weighted1)

    def arrival(n):
        source = origin(n)
        return pltpu.make_async_remote_copy(
            src_ref=send.at[source], dst_ref=got.at[source], send_sem=send_sem.at[source],
            recv_sem=got_sem.at[source], device_id=(source, plane), device_id_type=MESH,
        )

    def homeward(n):
        to = origin(n)
        return pltpu.make_async_remote_copy(
            src_ref=solved.at[to], dst_ref=returned.at[pl.ds(me * capacity, capacity)],
            send_sem=back_sem.at[to], recv_sem=home_sem.at[me], device_id=(to, plane), device_id_type=MESH,
        )

    def add_grid(weighted, row):
        total[...] += lax.dot_general(
            weighted[...], row[...], (((1,), (1,)), ((), ())), preferred_element_type=jnp.float32
        )

    def chunk(n, row, weighted, last_row, last_weighted):
        source = origin(n)
        arrival(n).wait_recv()

        def rec(k, which):
            return got[source, k, pl.ds(which, 1), :]

        def emit(k, part, value):
            solved[source, k, pl.ds(part, 1), :] = value

        add_grid(last_weighted, last_row)
        work_chunk(rec, model_t[...], table_ref[...], row, weighted, emit, capacity, side)

        @pl.when(n > 0)
        def _():
            homeward(n).start()

    def two(step, carry):
        chunk(2 * step, row0, weighted0, row1, weighted1)
        chunk(2 * step + 1, row1, weighted1, row0, weighted0)
        return carry

    lax.fori_loop(0, owners // 2, two, 0)
    add_grid(weighted1, row1)
    grids[plane] = total[...].T.astype(jnp.bfloat16)

    def pass_on(which, half, to, sem):
        piece = grids.at[which] if half is None else grids.at[which, pl.ds(half * side, side)]
        return pltpu.make_async_remote_copy(
            src_ref=piece, dst_ref=piece, send_sem=grid_send.at[sem], recv_sem=grid_got.at[sem],
            device_id=(me, to), device_id_type=MESH,
        )

    started = [
        pass_on(plane, 0, ahead, 0),
        pass_on(plane, 1, behind, 1),
        pass_on(plane, 1, ahead, 2),
        pass_on(plane, 0, behind, 3),
        pass_on(plane, None, sibling, 6),
    ]
    for copy in started:
        copy.start()

    def came(which, half, sem):
        pass_on(which, half, sibling, sem).wait_recv()

    def onward(which, half, to, sem):
        copy = pass_on(which, half, to, sem)
        copy.start()
        started.append(copy)

    came(behind, 0, 0)
    onward(behind, 0, ahead, 4)
    came(ahead, 1, 1)
    onward(ahead, 1, behind, 5)

    def collect(n, carry):
        source = target(n)
        pltpu.make_async_remote_copy(
            src_ref=solved.at[source], dst_ref=returned.at[pl.ds(source * capacity, capacity)],
            send_sem=back_sem.at[source], recv_sem=home_sem.at[source], device_id=(source, plane), device_id_type=MESH,
        ).wait_recv()
        return carry

    lax.fori_loop(1, owners, collect, 0)
    returned[pl.ds(me * capacity, capacity)] = solved[me]

    def unpack(b, carry):
        residual_out[b] = returned[index_s[owners * capacity // lanes, b]]
        return carry

    lax.fori_loop(0, blocks, unpack, 0, unroll=8)

    came(behind, 1, 2)
    onward(behind, None, sibling, 7)
    came(ahead, 0, 3)
    onward(ahead, None, sibling, 8)
    came(opposite, 0, 4)
    came(opposite, 1, 5)
    onward(opposite, None, sibling, 9)

    def flip(which):
        return which + 1 - 2 * core

    acc = None
    for which, sem in ((plane, None), (behind, None), (ahead, None), (opposite, None), (sibling, 6), (flip(behind), 7), (flip(ahead), 8), (flip(opposite), 9)):
        if sem is not None:
            came(which, None, sem)
        term = coupling_s[plane, which] * grids[which].astype(jnp.float32)
        coupled_out[...] = term if acc is None else coupled_out[...] + term
        acc = True

    def settle(n, carry):
        outward(n).wait_send()
        homeward(n).wait_send()
        return carry

    lax.fori_loop(1, owners, settle, 0)
    for copy in started:
        copy.wait_send()


def body(visibilities, uv_cell, sub_pixel, w_plane, block_tile, model_grid, kernel_table, coupling):
    blocks = visibilities.shape[1]
    rows = visibilities.shape[3]
    owners = lax.axis_size("tile")
    capacity = 3 * blocks // owners
    tiles, side = model_grid.shape[1], model_grid.shape[2]
    oversample, support = kernel_table.shape[1], kernel_table.shape[2]
    planes = lax.axis_size("freq")
    chips_x, chips_y = planes // 2, 4
    table = kernel_table.reshape(-1, support).T.astype(jnp.float32)
    vmem = pl.BlockSpec(memory_space=pltpu.VMEM)
    smem = pl.BlockSpec(memory_space=pltpu.SMEM)
    copies = pltpu.SemaphoreType.DMA
    taps = (tiles * side, capacity * rows)
    residuals, coupled = pl.pallas_call(
        functools.partial(kernel, (owners, capacity, tiles, side, oversample, chips_y, chips_x)),
        out_shape=(
            jax.ShapeDtypeStruct((blocks, 2, rows), jnp.float32),
            jax.ShapeDtypeStruct((tiles * side, 2 * side), jnp.float32),
        ),
        in_specs=[smem] * 3 + [vmem] * 6,
        out_specs=[vmem] * 2,
        scratch_shapes=[
            pltpu.VMEM((blocks + 1, 4, rows), jnp.float32),
            pltpu.VMEM((4, rows), jnp.int32),
            pltpu.SMEM((4, rows), jnp.int32),
            pltpu.VMEM((2 * side, tiles * side), jnp.bfloat16),
            pltpu.VMEM((owners, capacity, 4, rows), jnp.float32),
            pltpu.VMEM((owners, capacity, 4, rows), jnp.float32),
            pltpu.VMEM((owners, capacity, 2, rows), jnp.float32),
            pltpu.VMEM((owners * capacity, 2, rows), jnp.float32),
            pltpu.VMEM(taps, jnp.bfloat16),
            pltpu.VMEM(taps, jnp.bfloat16),
            pltpu.VMEM(taps, jnp.bfloat16),
            pltpu.VMEM(taps, jnp.bfloat16),
            pltpu.VMEM((2 * side, tiles * side), jnp.float32),
            pltpu.VMEM((planes, tiles * side, 2 * side), jnp.bfloat16),
            copies,
            copies((owners,)),
            copies((owners,)),
            copies((owners,)),
            copies((owners,)),
            copies((10,)),
            copies((10,)),
        ],
        compiler_params=pltpu.CompilerParams(collective_id=0, has_side_effects=True, vmem_limit_bytes=32 << 20),
    )(
        block_tile,
        w_plane,
        coupling,
        block_tile,
        visibilities[0],
        uv_cell[0],
        sub_pixel[0],
        model_grid.reshape(tiles * side, 2 * side),
        table,
    )
    return residuals[None], coupled.reshape(1, tiles, side, 2 * side)


def solution(mesh):
    return jax.shard_map(
        body,
        mesh=mesh,
        in_specs=(
            P("freq", "tile", None, None),
            P("freq", "tile", None, None),
            P("freq", "tile", None, None),
            P("freq", "tile"),
            P("freq", "tile"),
            P("freq", "tile", None, None),
            P(),
            P(),
        ),
        out_specs=(P("freq", "tile", None, None), P("freq", "tile", None, None)),
        check_vma=False,
    )
```

time: 116 us -> 58.4 us (0.50)
  waiting for transfers between devices: 35.9 us -> 0 us
  Pallas kernels: 30.8 us -> 51.9 us
  starting transfers between devices: 20.6 us -> 0 us
  between operations: 14.2 us -> 0.68 us
  other arithmetic: 9.78 us -> 0 us
  local copies, waits for them, and re-layouts: 4.21 us -> 5.65 us
    all_to_all x2 -> x0, waiting for transfers between devices: 29.6 us -> none  [the longest x1 18.9 us: body(): lax.all_to_all(sent.reshape(owners, capacity, 4, rows), 'tile', split_axi...]
    pallas_call x1, Pallas kernels: 30.8 us -> 51.9 us  [body(): pl.pallas_call(functools.partial(kernel, (owners, capacity, tiles, side,...]
    all_to_all x2 -> x0, starting transfers between devices: 20.5 us -> none  [the longest x1 12.2 us: body(): lax.all_to_all(sent.reshape(owners, capacity, 4, rows), 'tile', split_axi...]
    all_gather x1 -> x0, waiting for transfers between devices: 6.3 us -> none  [body(): lax.all_gather(grid_rounded, 'freq', axis=0, tiled=True).astype(jnp.float32)]
    select_n x5 -> x0, other arithmetic: 3.8 us -> none  [the longest x1 2.2 us: body(): jnp.where(filled[:, None, None], jnp.take(records, source, axis=0), empty)]
    unnamed x13 -> x16, local copies, waits for them, and re-layouts: 0.95 us -> 4.72 us
    gather x2 -> x0, local copies, waits for them, and re-layouts: 2.76 us -> none  [the longest x1 2.02 us: body(): jnp.take(records, source, axis=0)]
    reduce_sum x3 -> x0, other arithmetic: 2.54 us -> none  [the longest x1 2.22 us: body(): jnp.sum(own_row[:, None, None, None] * lax.all_gather(grid_rounded, 'freq...]
  transfers between devices with their start and end apart: 3 -> 0, of which waited for: 3 -> 0; matrix products, arithmetic and copies ran while one was open for 2% -> 0% of each run, Pallas kernels for 0% -> 0%
where the time goes in v2:
time: 58.4 us; the launch traced here: 58.2 us
  Pallas kernels  51.9 us (89%)
  local copies, waits for them, and re-layouts  5.65 us (10%)
  between operations  0.68 us (1%)
    pallas_call x1, Pallas kernels, body(): pl.pallas_call(functools.partial(kernel, (owners, capacity, tiles, side,...  51.9 us
    unnamed x16, local copies, waits for them, and re-layouts  4.72 us

profile of v2, /device:TPU:1, one launch (start us, length us, event | category | flops | bytes accessed | tf_op | source)
XLA Modules:
  0.0 58.2 jit_solution(1361532150175099471)
XLA Ops:
  0.6 0.0 copy-start
  0.6 0.8 %copy.11 = f32[16,8,8]{1,0,2:T(8,128)S(1)} copy(bf16[16,8,8]{0,2,1:T(8,128)(2,1)} %param.14) | data formatting | bytes 6144 | tf_op jit(solution)/shard_map/convert_element_type | solution.py:307
  1.5 0.0 copy-start.4
  1.5 0.1 reshape.15
  1.6 0.0 copy-start.5
  1.6 0.0 copy-start.6
  1.6 0.0 copy-done
  1.6 0.6 copy-done.4
  2.2 0.0 copy-done.5
  2.2 0.0 copy-done.6
  2.3 0.0 copy-start.1
  2.3 0.9 %copy-done.1 = s32[1,128,2,128]{3,2,1,0:T(2,128)S(1)} copy-done((s32[1,128,2,128]{3,2,1,0:T(2,128)S(1)}, s32[1,128,2,128]{3,2,1,0:T(2,128)}, u32[]{:S(2)}) %copy-start.1) | copy-done | bytes 131096
  3.2 0.0 copy-start.2
  3.2 0.9 %copy-done.2 = s32[1,128,2,128]{3,2,1,0:T(2,128)S(1)} copy-done((s32[1,128,2,128]{3,2,1,0:T(2,128)S(1)}, s32[1,128,2,128]{3,2,1,0:T(2,128)}, u32[]{:S(2)}) %copy-start.2) | copy-done | bytes 131096
  4.1 0.0 copy-start.3
  4.1 0.9 %copy-done.3 = bf16[1,2,128,256]{3,2,1,0:T(8,128)(2,1)S(1)} copy-done((bf16[1,2,128,256]{3,2,1,0:T(8,128)(2,1)S(1)}, bf16[1,2,128,256]{3,2,1,0:T(8,128)(2,1)}, u32[]{:S(2)}) %copy-start.3) | copy-done | bytes 131096
  5.0 51.9 %shard_map.95 = (f32[128,2,128]{2,1,0:T(2,128)S(1)}, f32[256,256]{1,0:T(8,128)S(1)}) custom-call(s32[1,128]{1,0:T(1,128)S(1)} %copy-done.5, s32[1,128]{1,0:T(1,128)S(1)} %copy-done.6, f32[8,8]{1,0:T(8,128)S(1)} %copy-done.4, s32[1,128]{1,0:T(1,128)S(1)} %copy-done.5, f32[128,2,128]{2,1,0:T(2,128)S(1)} %bitcast.10, s32[128,2,128]{2,1,0:T(2,128)S(1)} %bitcast.11, ...), custom_call_target="tpu_custom_call" | custom-call | tf_op jit(solution)/shard_map/pallas_call | solution.py:312
  56.8 0.7 %copy.14 = f32[1,128,2,128]{3,2,1,0:T(2,128)} copy(f32[1,128,2,128]{3,2,1,0:T(2,128)S(1)} %bitcast.14) | data formatting | bytes 262144
  57.5 0.7 %copy.15 = f32[1,2,128,256]{3,2,1,0:T(8,128)} copy(f32[1,2,128,256]{3,2,1,0:T(8,128)S(1)} %bitcast.9) | data formatting | bytes 524288
Async XLA Ops:
  0.6 1.0 %copy-start = (f32[1,128,2,128]{3,2,1,0:T(2,128)S(1)}, f32[1,128,2,128]{3,2,1,0:T(2,128)}, u32[]{:S(2)}) copy-start(f32[1,128,2,128]{3,2,1,0:T(2,128)} %param.8) | copy-start | bytes 393220
  1.5 0.7 %copy-start.4 = (f32[8,8]{1,0:T(8,128)S(1)}, f32[8,8]{1,0:T(8,128)}, u32[]{:S(2)}) copy-start(f32[8,8]{1,0:T(8,128)} %coupling_s.1) | copy-start | bytes 772
  1.6 0.7 %copy-start.5 = (s32[1,128]{1,0:T(1,128)S(1)}, s32[1,128]{1,0:T(1,128)}, u32[]{:S(2)}) copy-start(s32[1,128]{1,0:T(1,128)} %tile_v.1) | copy-start | bytes 1540
  1.6 0.7 %copy-start.6 = (s32[1,128]{1,0:T(1,128)S(1)}, s32[1,128]{1,0:T(1,128)}, u32[]{:S(2)}) copy-start(s32[1,128]{1,0:T(1,128)} %plane_s.1) | copy-start | bytes 1540
  2.3 0.9 %copy-start.1 = (s32[1,128,2,128]{3,2,1,0:T(2,128)S(1)}, s32[1,128,2,128]{3,2,1,0:T(2,128)}, u32[]{:S(2)}) copy-start(s32[1,128,2,128]{3,2,1,0:T(2,128)} %param.9) | copy-start | bytes 393220
  3.2 0.9 %copy-start.2 = (s32[1,128,2,128]{3,2,1,0:T(2,128)S(1)}, s32[1,128,2,128]{3,2,1,0:T(2,128)}, u32[]{:S(2)}) copy-start(s32[1,128,2,128]{3,2,1,0:T(2,128)} %param.10) | copy-start | bytes 393220
  4.1 0.9 %copy-start.3 = (bf16[1,2,128,256]{3,2,1,0:T(8,128)(2,1)S(1)}, bf16[1,2,128,256]{3,2,1,0:T(8,128)(2,1)}, u32[]{:S(2)}) copy-start(bf16[1,2,128,256]{3,2,1,0:T(8,128)(2,1)} %param.13) | copy-start | bytes 393220

commit v3 on v2

--- a/solution.py
+++ b/solution.py
@@ -69,39 +69,69 @@
 
 def kernel(
     dims,
-    tile_s, plane_s, coupling_s, tile_v, samples, cells, offsets, model, table_ref,
+    tile_h, plane_h, coupling_h, samples_h, cells_h, offsets_h, model_h, table_h,
     residual_out, coupled_out,
-    records, index_v, index_s, model_t, send, got, solved, returned,
+    tile_s, plane_s, tile_v, coupling_v, samples, cells, offsets, model, table_raw, table_ref,
+    records, index_v, index_s, model_t, send, got, solved, returned, relayed, rehomed,
     row0, row1, weighted0, weighted1, total, grids,
-    index_sem, send_sem, got_sem, back_sem, home_sem, grid_send, grid_got,
+    load_sem, index_sem, send_sem, got_sem, back_sem, home_sem, grid_send, grid_got,
+    relay_send, relay_got, relay_on, rehome_send, rehome_got, rehome_on,
 ):
     owners, capacity, tiles, side, oversample, chips_y, chips_x = dims
     chips_z = owners // chips_y
+    half_z, quarter_z = chips_z // 2, chips_z // 4
     blocks = samples.shape[0]
     lanes = 128
     me = lax.axis_index("tile")
     plane = lax.axis_index("freq")
     mine_y, mine_z = me // chips_z, lax.rem(me, chips_z)
     mine_x, core = plane // 2, lax.rem(plane, 2)
+    far_group = chips_z - 3
+    relays = [(far_group * chips_y + across, across) for across in range(1, 1)]
+
+    def place(y, z):
+        return lax.rem(mine_y + y + chips_y, chips_y) * chips_z + lax.rem(mine_z + z + chips_z, chips_z)
 
     def hop(n):
         group, across = n // chips_y, lax.rem(n, chips_y)
-        along = (group + 1) // 2 * (2 * lax.rem(group, 2) - 1)
-        return across, along
+        past = group // (far_group + 1)
+        far = group // far_group - past
+        turn = group - past
+        near = (turn + 1) // 2 * (2 * lax.rem(turn, 2) - 1)
+        return across, near * (1 - far) + half_z * far
 
     def target(n):
         across, along = hop(n)
-        return lax.rem(mine_y + across, chips_y) * chips_z + lax.rem(mine_z + along + chips_z, chips_z)
+        return place(across, along)
 
     def origin(n):
         across, along = hop(n)
-        return lax.rem(mine_y - across + chips_y, chips_y) * chips_z + lax.rem(mine_z - along + chips_z, chips_z)
+        return place(-across, -along)
 
     sibling = 2 * mine_x + 1 - core
     ahead = 2 * lax.rem(mine_x + 1, chips_x) + core
     behind = 2 * lax.rem(mine_x + chips_x - 1, chips_x) + core
     opposite = 2 * lax.rem(mine_x + 2, chips_x) + core
 
+    loads = [
+        pltpu.make_async_copy(source, to, load_sem.at[i])
+        for i, (source, to) in enumerate(
+            (
+                (tile_h, tile_v),
+                (tile_h, tile_s),
+                (plane_h, plane_s),
+                (cells_h, cells),
+                (offsets_h, offsets),
+                (samples_h, samples),
+                (table_h, table_raw),
+                (model_h, model),
+                (coupling_h, coupling_v),
+            )
+        )
+    ]
+    for load in loads:
+        load.start()
+
     barrier = pltpu.get_barrier_semaphore()
 
     def greet(n, carry):
@@ -112,6 +142,7 @@
     for other in (sibling, ahead, behind):
         pl.semaphore_signal(barrier, inc=1, device_id=(me, other), device_id_type=MESH)
 
+    loads[0].wait()
     owner = lax.shift_right_logical(tile_v[...], tiles.bit_length() - 1)
     wide = (blocks, lanes)
     down = lax.broadcasted_iota(jnp.int32, wide, 0)
@@ -130,15 +161,17 @@
     index_v[pl.ds(owners * capacity // lanes, 1), :] = slot
     index_copy = pltpu.make_async_copy(index_v, index_s, index_sem)
     index_copy.start()
+    for load in loads[1:6]:
+        load.wait()
 
     def fill(b, carry):
         tile = lax.rem(tile_s[0, b], tiles)
-        base = plane_s[0, b] * oversample
+        kernel_plane = plane_s[0, b]
         records[b, pl.ds(0, 2), :] = samples[b]
-        place = (cells[b, pl.ds(0, 1), :] + tile * side) * SHIFT + cells[b, pl.ds(1, 1), :]
-        lookup = (offsets[b, pl.ds(0, 1), :] + base) * SHIFT + offsets[b, pl.ds(1, 1), :] + base
-        records[b, pl.ds(2, 1), :] = place.astype(jnp.float32)
-        records[b, pl.ds(3, 1), :] = lookup.astype(jnp.float32)
+        spot = (cells[b, pl.ds(0, 1), :] + tile * side) * SHIFT + cells[b, pl.ds(1, 1), :]
+        lookup = offsets[b] * (lanes // oversample) + kernel_plane
+        records[b, pl.ds(2, 1), :] = spot.astype(jnp.float32)
+        records[b, pl.ds(3, 1), :] = (lookup[0:1] * SHIFT + lookup[1:2]).astype(jnp.float32)
         return carry
 
     lax.fori_loop(0, blocks, fill, 0, unroll=8)
@@ -146,48 +179,92 @@
         lax.broadcasted_iota(jnp.int32, (4, lanes), 0) == 2, jnp.float32(tiles * side * SHIFT), jnp.float32(0)
     )
     index_copy.wait()
-    pl.semaphore_wait(barrier, owners + 2)
-
-    def outward(n):
-        to = target(n)
-        return pltpu.make_async_remote_copy(
-            src_ref=send.at[to], dst_ref=got.at[me], send_sem=send_sem.at[to], recv_sem=got_sem.at[me],
-            device_id=(to, plane), device_id_type=MESH,
-        )
-
-    def pack(to):
+
+    def pack(to, carry):
         for j in range(capacity):
             s = to * capacity + j
             send[to, j] = records[index_s[s // lanes, lax.rem(s, lanes)]]
-
-    def dispatch(n, carry):
-        pack(target(n))
-        outward(n).start()
-        return carry
-
-    lax.fori_loop(1, owners, dispatch, 0)
-    pack(me)
+        return carry
+
+    lax.fori_loop(0, owners, pack, 0)
     own = pltpu.make_async_copy(send.at[me], got.at[me], got_sem.at[me])
     own.start()
+    pl.semaphore_wait(barrier, owners + 2)
+
+    def each_direct(act):
+        def visit(n, carry):
+            direct = n > 0
+            for relay, _ in relays:
+                direct = direct & (n != relay)
+
+            @pl.when(direct)
+            def _():
+                act(n)
+
+            return carry
+
+        lax.fori_loop(1, owners, visit, 0)
+
+    def outward(n):
+        to = target(n)
+        return pltpu.make_async_remote_copy(
+            src_ref=send.at[to], dst_ref=got.at[me], send_sem=send_sem.at[to], recv_sem=got_sem.at[me],
+            device_id=(to, plane), device_id_type=MESH,
+        )
+
+    def arrival(n):
+        source = origin(n)
+        return pltpu.make_async_remote_copy(
+            src_ref=send.at[source], dst_ref=got.at[source], send_sem=send_sem.at[source],
+            recv_sem=got_sem.at[source], device_id=(source, plane), device_id_type=MESH,
+        )
+
+    def homeward(n):
+        to = origin(n)
+        return pltpu.make_async_remote_copy(
+            src_ref=solved.at[to], dst_ref=returned.at[pl.ds(me * capacity, capacity)],
+            send_sem=back_sem.at[to], recv_sem=home_sem.at[me], device_id=(to, plane), device_id_type=MESH,
+        )
+
+    def relay_out(i):
+        return pltpu.make_async_remote_copy(
+            src_ref=send.at[place(relays[i][1], half_z)], dst_ref=relayed.at[i], send_sem=relay_send.at[i],
+            recv_sem=relay_got.at[i], device_id=(place(0, -quarter_z), plane), device_id_type=MESH,
+        )
+
+    def relay_onward(i):
+        source = place(0, quarter_z)
+        return pltpu.make_async_remote_copy(
+            src_ref=relayed.at[i], dst_ref=got.at[source], send_sem=relay_on.at[i], recv_sem=got_sem.at[source],
+            device_id=(place(relays[i][1], -quarter_z), plane), device_id_type=MESH,
+        )
+
+    def rehome_out(i):
+        return pltpu.make_async_remote_copy(
+            src_ref=solved.at[place(-relays[i][1], half_z)], dst_ref=rehomed.at[i], send_sem=rehome_send.at[i],
+            recv_sem=rehome_got.at[i], device_id=(place(0, -quarter_z), plane), device_id_type=MESH,
+        )
+
+    def rehome_onward(i):
+        keeper = place(0, quarter_z)
+        return pltpu.make_async_remote_copy(
+            src_ref=rehomed.at[i], dst_ref=returned.at[pl.ds(keeper * capacity, capacity)],
+            send_sem=rehome_on.at[i], recv_sem=home_sem.at[keeper],
+            device_id=(place(-relays[i][1], -quarter_z), plane), device_id_type=MESH,
+        )
+
+    for i in range(len(relays)):
+        relay_out(i).start()
+    each_direct(lambda n: outward(n).start())
+    for load in loads[6:]:
+        load.wait()
+    for which in range(oversample):
+        table_ref[:, pl.ds(which * (lanes // oversample), lanes // oversample)] = table_raw[which].astype(jnp.float32)
     model_t[...] = model[...].T
     total[...] = jnp.zeros_like(total)
     row1[...] = jnp.zeros_like(row1)
     weighted1[...] = jnp.zeros_like(weighted1)
 
-    def arrival(n):
-        source = origin(n)
-        return pltpu.make_async_remote_copy(
-            src_ref=send.at[source], dst_ref=got.at[source], send_sem=send_sem.at[source],
-            recv_sem=got_sem.at[source], device_id=(source, plane), device_id_type=MESH,
-        )
-
-    def homeward(n):
-        to = origin(n)
-        return pltpu.make_async_remote_copy(
-            src_ref=solved.at[to], dst_ref=returned.at[pl.ds(me * capacity, capacity)],
-            send_sem=back_sem.at[to], recv_sem=home_sem.at[me], device_id=(to, plane), device_id_type=MESH,
-        )
-
     def add_grid(weighted, row):
         total[...] += lax.dot_general(
             weighted[...], row[...], (((1,), (1,)), ((), ())), preferred_element_type=jnp.float32
@@ -205,12 +282,31 @@
 
         add_grid(last_weighted, last_row)
         work_chunk(rec, model_t[...], table_ref[...], row, weighted, emit, capacity, side)
-
-        @pl.when(n > 0)
+        direct = n > 0
+        for i, (relay, _) in enumerate(relays):
+            direct = direct & (n != relay)
+
+            @pl.when(n == relay)
+            def _(i=i):
+                rehome_out(i).start()
+
+        @pl.when(direct)
         def _():
             homeward(n).start()
 
     def two(step, carry):
+        @pl.when(step == 2)
+        def _():
+            for i in range(len(relays)):
+                relay_out(i).wait_recv()
+                relay_onward(i).start()
+
+        @pl.when(step == owners // 2 - 2)
+        def _():
+            for i in range(len(relays)):
+                rehome_out(i).wait_recv()
+                rehome_onward(i).start()
+
         chunk(2 * step, row0, weighted0, row1, weighted1)
         chunk(2 * step + 1, row1, weighted1, row0, weighted0)
         return carry
@@ -277,20 +373,26 @@
     def flip(which):
         return which + 1 - 2 * core
 
-    acc = None
-    for which, sem in ((plane, None), (behind, None), (ahead, None), (opposite, None), (sibling, 6), (flip(behind), 7), (flip(ahead), 8), (flip(opposite), 9)):
-        if sem is not None:
-            came(which, None, sem)
-        term = coupling_s[plane, which] * grids[which].astype(jnp.float32)
-        coupled_out[...] = term if acc is None else coupled_out[...] + term
-        acc = True
-
-    def settle(n, carry):
+    share = coupling_v[pl.ds(plane, 1), :]
+    number = lax.broadcasted_iota(jnp.int32, share.shape, 1)
+
+    def term(which):
+        part = jnp.sum(jnp.where(number == which, share, 0.0), axis=1, keepdims=True)
+        return part * grids[which].astype(jnp.float32)
+
+    coupled_out[...] = term(plane) + term(behind) + term(ahead) + term(opposite)
+    for which, sem in ((sibling, 6), (flip(behind), 7), (flip(ahead), 8), (flip(opposite), 9)):
+        came(which, None, sem)
+    coupled_out[...] += term(sibling) + term(flip(behind)) + term(flip(ahead)) + term(flip(opposite))
+
+    def settle(n):
         outward(n).wait_send()
         homeward(n).wait_send()
-        return carry
-
-    lax.fori_loop(1, owners, settle, 0)
+
+    each_direct(settle)
+    for i in range(len(relays)):
+        for copy in (relay_out(i), relay_onward(i), rehome_out(i), rehome_onward(i)):
+            copy.wait_send()
     for copy in started:
         copy.wait_send()
 
@@ -301,23 +403,42 @@
     owners = lax.axis_size("tile")
     capacity = 3 * blocks // owners
     tiles, side = model_grid.shape[1], model_grid.shape[2]
-    oversample, support = kernel_table.shape[1], kernel_table.shape[2]
+    oversample = kernel_table.shape[1]
     planes = lax.axis_size("freq")
     chips_x, chips_y = planes // 2, 4
-    table = kernel_table.reshape(-1, support).T.astype(jnp.float32)
     vmem = pl.BlockSpec(memory_space=pltpu.VMEM)
-    smem = pl.BlockSpec(memory_space=pltpu.SMEM)
+    hbm = pl.BlockSpec(memory_space=pltpu.HBM)
     copies = pltpu.SemaphoreType.DMA
     taps = (tiles * side, capacity * rows)
+    operands = (
+        block_tile,
+        w_plane,
+        coupling,
+        visibilities[0],
+        uv_cell[0],
+        sub_pixel[0],
+        model_grid.reshape(tiles * side, 2 * side),
+        kernel_table.transpose(1, 2, 0),
+    )
     residuals, coupled = pl.pallas_call(
         functools.partial(kernel, (owners, capacity, tiles, side, oversample, chips_y, chips_x)),
         out_shape=(
             jax.ShapeDtypeStruct((blocks, 2, rows), jnp.float32),
             jax.ShapeDtypeStruct((tiles * side, 2 * side), jnp.float32),
         ),
-        in_specs=[smem] * 3 + [vmem] * 6,
+        in_specs=[hbm] * len(operands),
         out_specs=[vmem] * 2,
         scratch_shapes=[
+            pltpu.SMEM((1, blocks), jnp.int32),
+            pltpu.SMEM((1, blocks), jnp.int32),
+            pltpu.VMEM((1, blocks), jnp.int32),
+            pltpu.VMEM((planes, planes), jnp.float32),
+            pltpu.VMEM((blocks, 2, rows), jnp.float32),
+            pltpu.VMEM((blocks, 2, rows), jnp.int32),
+            pltpu.VMEM((blocks, 2, rows), jnp.int32),
+            pltpu.VMEM((tiles * side, 2 * side), jnp.bfloat16),
+            pltpu.VMEM(operands[-1].shape, jnp.bfloat16),
+            pltpu.VMEM((8, rows), jnp.float32),
             pltpu.VMEM((blocks + 1, 4, rows), jnp.float32),
             pltpu.VMEM((4, rows), jnp.int32),
             pltpu.SMEM((4, rows), jnp.int32),
@@ -326,12 +447,15 @@
             pltpu.VMEM((owners, capacity, 4, rows), jnp.float32),
             pltpu.VMEM((owners, capacity, 2, rows), jnp.float32),
             pltpu.VMEM((owners * capacity, 2, rows), jnp.float32),
+            pltpu.VMEM((2, capacity, 4, rows), jnp.float32),
+            pltpu.VMEM((2, capacity, 2, rows), jnp.float32),
             pltpu.VMEM(taps, jnp.bfloat16),
             pltpu.VMEM(taps, jnp.bfloat16),
             pltpu.VMEM(taps, jnp.bfloat16),
             pltpu.VMEM(taps, jnp.bfloat16),
             pltpu.VMEM((2 * side, tiles * side), jnp.float32),
             pltpu.VMEM((planes, tiles * side, 2 * side), jnp.bfloat16),
+            copies((len(operands) + 1,)),
             copies,
             copies((owners,)),
             copies((owners,)),
@@ -339,19 +463,15 @@
             copies((owners,)),
             copies((10,)),
             copies((10,)),
+            copies((2,)),
+            copies((2,)),
+            copies((2,)),
+            copies((2,)),
+            copies((2,)),
+            copies((2,)),
         ],
-        compiler_params=pltpu.CompilerParams(collective_id=0, has_side_effects=True, vmem_limit_bytes=32 << 20),
-    )(
-        block_tile,
-        w_plane,
-        coupling,
-        block_tile,
-        visibilities[0],
-        uv_cell[0],
-        sub_pixel[0],
-        model_grid.reshape(tiles * side, 2 * side),
-        table,
-    )
+        compiler_params=pltpu.CompilerParams(collective_id=0, has_side_effects=True, vmem_limit_bytes=40 << 20),
+    )(*(pltpu.with_memory_space_constraint(operand, pltpu.HBM) for operand in operands))
     return residuals[None], coupled.reshape(1, tiles, side, 2 * side)
 
 

time: 58.4 us -> 54.1 us (0.926)
  local copies, waits for them, and re-layouts: 5.65 us -> 1.36 us
    unnamed x16 -> x2, local copies, waits for them, and re-layouts: 4.72 us -> 1.36 us
    convert_element_type x2 -> x0, local copies, waits for them, and re-layouts: 0.93 us -> none  [body(): table = kernel_table.reshape(-1, support).T.astype(jnp.float32)]
where the time goes in v3:
time: 54.1 us; the launch traced here: 54 us
  Pallas kernels  52 us (96%)
  local copies, waits for them, and re-layouts  1.36 us (3%)
  between operations  0.64 us (1%)
    pallas_call x1, Pallas kernels, body(): pl.pallas_call(functools.partial(kernel, (owners, capacity, tiles, side,...  52 us
    unnamed x2, local copies, waits for them, and re-layouts  1.36 us

profile of v3, /device:TPU:1, one launch (start us, length us, event | category | flops | bytes accessed | tf_op | source)
XLA Modules:
  0.0 54.0 jit_solution(13620890670133629313)
XLA Ops:
  0.6 52.0 %shard_map.95 = (f32[128,2,128]{2,1,0:T(2,128)S(1)}, f32[256,256]{1,0:T(8,128)S(1)}) custom-call(s32[1,128]{1,0:T(1,128)} %tile_h.1, s32[1,128]{1,0:T(1,128)} %plane_h.1, f32[8,8]{1,0:T(8,128)} %coupling_h.1, f32[128,2,128]{2,1,0:T(2,128)} %bitcast.9, s32[128,2,128]{2,1,0:T(2,128)} %bitcast.10, s32[128,2,128]{2,1,0:T(2,128)} %bitcast.11, ...), custom_call_target="tpu_custom_call" | custom-call | tf_op jit(solution)/shard_map/pallas_call | solution.py:423
  52.6 0.7 %copy.12 = f32[1,128,2,128]{3,2,1,0:T(2,128)} copy(f32[1,128,2,128]{3,2,1,0:T(2,128)S(1)} %bitcast.8) | data formatting | bytes 262144
  53.3 0.7 %copy.13 = f32[1,2,128,256]{3,2,1,0:T(8,128)} copy(f32[1,2,128,256]{3,2,1,0:T(8,128)S(1)} %bitcast.7) | data formatting | bytes 524288

commit v4 on v3

v4 whole, which is shorter than its diff:
```python
import functools

import jax
import jax.numpy as jnp
from jax import lax
from jax.experimental import pallas as pl
from jax.experimental.pallas import tpu as pltpu
from jax.sharding import PartitionSpec as P

SHIFT = 65536
LEVELS = 32767.0
PIECES = 4
SAMPLE_FRACTION = 2.0**24
MODEL_FRACTION = 2.0**23


def spread(start, table_row, table, lanes):
    sub = lax.broadcasted_iota(jnp.int32, (8, lanes), 0)
    taps = jnp.take_along_axis(table, jnp.broadcast_to(table_row, (8, lanes)), axis=1, mode="promise_in_bounds")
    offset = sub - start
    folded = jnp.take_along_axis(taps, jnp.bitwise_and(offset, 7), axis=0, mode="promise_in_bounds")
    return folded, lax.shift_right_arithmetic(offset, 3)


def twice(folded, group):
    values = jnp.concatenate([folded, folded], axis=0).astype(jnp.bfloat16)
    groups = jnp.concatenate([group, group + 1], axis=0).astype(jnp.float32).astype(jnp.bfloat16)
    return values, groups


def measure(values, fraction):
    while values.ndim > 2:
        values = jnp.max(values, axis=0)
    return jnp.floor(jnp.max(values, keepdims=True) * fraction).astype(jnp.int32) + 1


def encode(first, second, gain):
    high, low = (jnp.floor(value * gain + 0.5).astype(jnp.int32) for value in (first, second))
    return lax.shift_left(high, 16) | jnp.bitwise_and(low, SHIFT - 1)


def decode(word, scale, fraction):
    gain = scale.astype(jnp.float32) * (1.0 / (LEVELS * fraction))
    high = lax.shift_right_arithmetic(word, 16)
    low = lax.shift_right_arithmetic(lax.shift_left(word, 16), 16)
    return high.astype(jnp.float32) * gain, low.astype(jnp.float32) * gain


def work_chunk(message, model_t, table, row_ref, weighted_ref, model_ref, capacity, side):
    lanes = 128
    zero16 = jnp.zeros((16, lanes), jnp.bfloat16)
    samples = decode(message[pl.ds(0, capacity), :], message[pl.ds(3 * capacity, 1), :], SAMPLE_FRACTION)
    column = []
    for k in range(capacity):
        position = message[pl.ds(capacity + k, 1), :]
        lookup = message[pl.ds(2 * capacity + k, 1), :]
        folded, group = spread(lax.shift_right_logical(position, 16), lax.shift_right_logical(lookup, 16), table, lanes)
        values, groups = twice(folded, group)
        for tile in range(2 * side // 16):
            row_ref[pl.ds(16 * tile, 16), pl.ds(k * lanes, lanes)] = jnp.where(
                groups == jnp.bfloat16(-2 * tile), values, zero16
            )
        column.append(
            spread(jnp.bitwise_and(position, SHIFT - 1), jnp.bitwise_and(lookup, SHIFT - 1), table, lanes)
        )
    for pair in range(capacity // 2):
        partial = jnp.dot(
            model_t, row_ref[:, pl.ds(pair * 2 * lanes, 2 * lanes)], preferred_element_type=jnp.float32
        )
        for half in range(2):
            k = 2 * pair + half
            folded, group = column[k]
            block = partial[:, half * lanes : (half + 1) * lanes]
            picked = [jnp.zeros((8, lanes), jnp.float32)] * 2
            for tile in range(side // 8):
                hit = group == -tile
                for part in range(2):
                    start = part * side + 8 * tile
                    picked[part] = jnp.where(hit, block[start : start + 8], picked[part])
            for part in range(2):
                degridded = jnp.sum(picked[part] * folded, axis=0, keepdims=True)
                model_ref[pl.ds(part * 16 + k, 1), :] = degridded
                residual = samples[part][k : k + 1] - degridded
                values, groups = twice(residual * folded, group)
                for tile in range(side // 16):
                    weighted_ref[pl.ds(part * side + 16 * tile, 16), pl.ds(k * lanes, lanes)] = jnp.where(
                        groups == jnp.bfloat16(-2 * tile), values, zero16
                    )


MESH = pl.DeviceIdType.MESH


def kernel(
    dims,
    tile_h, plane_h, coupling_h, samples_h, cells_h, offsets_h, model_h, table_h,
    residual_out, coupled_out,
    tile_s, plane_s, tile_v, coupling_v, samples, cells, offsets, model, table_raw, table_ref,
    records, index_v, index_s, modelled, model_t, send, got, solved, returned,
    row0, row1, weighted0, weighted1, total, grids,
    load_sem, index_sem, send_sem, got_sem, back_sem, home_sem, grid_send, grid_got,
):
    owners, capacity, tiles, side, oversample, chips_y, chips_x = dims
    chips_z = owners // chips_y
    half_z = chips_z // 2
    blocks = samples_h.shape[0]
    lanes = 128
    out_rows, back_rows = 3 * capacity + 1, capacity + 1
    me = lax.axis_index("tile")
    plane = lax.axis_index("freq")
    mine_y, mine_z = me // chips_z, lax.rem(me, chips_z)
    mine_x, core = plane // 2, lax.rem(plane, 2)
    far_group = chips_z - 3

    def place(y, z):
        return lax.rem(mine_y + y + chips_y, chips_y) * chips_z + lax.rem(mine_z + z + chips_z, chips_z)

    def hop(n):
        group, across = n // chips_y, lax.rem(n, chips_y)
        past = group // (far_group + 1)
        far = group // far_group - past
        turn = group - past
        near = (turn + 1) // 2 * (2 * lax.rem(turn, 2) - 1)
        return across, near * (1 - far) + half_z * far

    def target(n):
        across, along = hop(n)
        return place(across, along)

    def origin(n):
        across, along = hop(n)
        return place(-across, -along)

    sibling = 2 * mine_x + 1 - core
    ahead = 2 * lax.rem(mine_x + 1, chips_x) + core
    behind = 2 * lax.rem(mine_x + chips_x - 1, chips_x) + core
    opposite = 2 * lax.rem(mine_x + 2, chips_x) + core

    loads = [
        pltpu.make_async_copy(source, to, load_sem.at[i])
        for i, (source, to) in enumerate(
            (
                (tile_h, tile_v),
                (tile_h, tile_s),
                (plane_h, plane_s),
                (cells_h, cells),
                (offsets_h, offsets),
                (samples_h, samples),
                (table_h, table_raw),
                (model_h, model),
                (coupling_h, coupling_v),
            )
        )
    ]
    for load in loads:
        load.start()

    barrier = pltpu.get_barrier_semaphore()

    def greet(n, carry):
        pl.semaphore_signal(barrier, inc=1, device_id=(target(n), plane), device_id_type=MESH)
        return carry

    lax.fori_loop(1, owners, greet, 0)
    for other in (sibling, ahead, behind):
        pl.semaphore_signal(barrier, inc=1, device_id=(me, other), device_id_type=MESH)

    loads[0].wait()
    owner = lax.shift_right_logical(tile_v[...], tiles.bit_length() - 1)
    wide = (blocks, lanes)
    down = lax.broadcasted_iota(jnp.int32, wide, 0)
    over = lax.broadcasted_iota(jnp.int32, wide, 1)

    def stand(row):
        return jnp.broadcast_to(row.astype(jnp.float32), wide).T.astype(jnp.int32)

    same = (stand(owner) == owner) & (down < over)
    slot = owner * capacity + jnp.sum(same.astype(jnp.int32), axis=0, keepdims=True)
    slots = stand(slot)
    for part in range(owners * capacity // lanes):
        index_v[pl.ds(part, 1), :] = blocks + jnp.sum(
            jnp.where(slots == over + part * lanes, down - blocks, 0), axis=0, keepdims=True
        )
    index_v[pl.ds(3, 1), :] = owner
    index_v[pl.ds(5, 3), :] = jnp.zeros((3, lanes), jnp.int32)
    index_v[pl.ds(4, 1), :] = slot - owner * capacity
    index_copy = pltpu.make_async_copy(index_v, index_s, index_sem)
    index_copy.start()
    for load in loads[1:6]:
        load.wait()

    scale = measure(jnp.abs(samples[...]), SAMPLE_FRACTION)
    gain = (LEVELS * SAMPLE_FRACTION) / scale.astype(jnp.float32)
    scale_row = jnp.broadcast_to(scale, (1, lanes))

    def fill(b, carry):
        tile = lax.rem(tile_s[0, b], tiles)
        kernel_plane = plane_s[0, b]
        spot = (cells[b, pl.ds(0, 1), :] + tile * side) * SHIFT + cells[b, pl.ds(1, 1), :]
        lookup = offsets[b] * (lanes // oversample) + kernel_plane
        records[b, pl.ds(0, 1), :] = encode(samples[b, pl.ds(0, 1), :], samples[b, pl.ds(1, 1), :], gain)
        records[b, pl.ds(1, 1), :] = spot
        records[b, pl.ds(2, 1), :] = lookup[0:1] * SHIFT + lookup[1:2]
        return carry

    lax.fori_loop(0, blocks, fill, 0, unroll=8)
    records[blocks, pl.ds(0, 3), :] = jnp.where(
        lax.broadcasted_iota(jnp.int32, (3, lanes), 0) == 1, tiles * side * SHIFT, 0
    )
    index_copy.wait()

    def outgoing(to):
        return send.at[to, pl.ds(0, out_rows)]

    def incoming(source):
        return got.at[source, pl.ds(0, out_rows)]

    def pack(to, carry):
        for j in range(capacity):
            s = to * capacity + j
            source = index_s[s // lanes, lax.rem(s, lanes)]
            send[to, pl.ds(j, 3, stride=capacity), :] = records[source, pl.ds(0, 3), :]
        send[to, pl.ds(3 * capacity, 1), :] = scale_row
        return carry

    lax.fori_loop(0, owners, pack, 0)
    own = pltpu.make_async_copy(outgoing(me), incoming(me), got_sem.at[me])
    own.start()
    pl.semaphore_wait(barrier, owners + 2)

    def each_partner(act):
        def visit(n, carry):
            act(n)
            return carry

        lax.fori_loop(1, owners, visit, 0)

    def outward(n):
        to = target(n)
        return pltpu.make_async_remote_copy(
            src_ref=outgoing(to), dst_ref=incoming(me), send_sem=send_sem.at[to], recv_sem=got_sem.at[me],
            device_id=(to, plane), device_id_type=MESH,
        )

    def arrival(n):
        source = origin(n)
        return pltpu.make_async_remote_copy(
            src_ref=outgoing(source), dst_ref=incoming(source), send_sem=send_sem.at[source],
            recv_sem=got_sem.at[source], device_id=(source, plane), device_id_type=MESH,
        )

    def homeward(n):
        to = origin(n)
        return pltpu.make_async_remote_copy(
            src_ref=solved.at[to, pl.ds(0, back_rows)], dst_ref=returned.at[me, pl.ds(0, back_rows)],
            send_sem=back_sem.at[to], recv_sem=home_sem.at[me], device_id=(to, plane), device_id_type=MESH,
        )

    each_partner(lambda n: outward(n).start())
    for load in loads[6:]:
        load.wait()
    for which in range(oversample):
        table_ref[:, pl.ds(which * (lanes // oversample), lanes // oversample)] = table_raw[which].astype(jnp.float32)
    model_t[...] = model[...].T
    total[...] = jnp.zeros_like(total)
    row1[...] = jnp.zeros_like(row1)
    weighted1[...] = jnp.zeros_like(weighted1)

    def add_grid(weighted, row):
        total[...] += lax.dot_general(
            row[...], weighted[...], (((1,), (1,)), ((), ())), preferred_element_type=jnp.float32
        )

    def chunk(n, turn, row, weighted, last_row, last_weighted):
        source = origin(n)
        add_grid(last_weighted, last_row)
        work_chunk(got.at[source], model_t[...], table_ref[...], row, weighted, modelled.at[turn], capacity, side)
        real, imaginary = modelled[turn, pl.ds(0, capacity), :], modelled[turn, pl.ds(16, capacity), :]
        here = measure(jnp.maximum(jnp.abs(real), jnp.abs(imaginary)), MODEL_FRACTION)
        solved[source, pl.ds(0, capacity), :] = encode(
            real, imaginary, (LEVELS * MODEL_FRACTION) / here.astype(jnp.float32)
        )
        solved[source, pl.ds(capacity, 1), :] = jnp.broadcast_to(here, (1, lanes))

    def group(step, carry):
        first = chips_y * step
        for across in range(chips_y):
            arrival(first + across).wait_recv()
        for across in range(0, chips_y, 2):
            chunk(first + across, across, row0, weighted0, row1, weighted1)
            chunk(first + across + 1, across + 1, row1, weighted1, row0, weighted0)

        @pl.when(step > 0)
        def _():
            homeward(first).start()

        for across in range(1, chips_y):
            homeward(first + across).start()
        return carry

    lax.fori_loop(0, chips_z, group, 0)
    add_grid(weighted1, row1)

    piece_rows = tiles * side // PIECES
    half = PIECES // 2

    def pass_on(which, piece, to, route):
        part = grids.at[which, pl.ds(piece * piece_rows, piece_rows)]
        return pltpu.make_async_remote_copy(
            src_ref=part, dst_ref=part, send_sem=grid_send.at[route, piece], recv_sem=grid_got.at[route, piece],
            device_id=(me, to), device_id_type=MESH,
        )

    started = []

    def launch(which, piece, to, route):
        copy = pass_on(which, piece, to, route)
        copy.start()
        started.append(copy)

    def came(which, piece, route):
        pass_on(which, piece, sibling, route).wait_recv()

    for piece in range(PIECES):
        spot = pl.ds(piece * piece_rows, piece_rows)
        grids[plane, spot, :] = total[spot, :].astype(jnp.bfloat16)
    for piece in range(PIECES):
        launch(plane, piece, ahead, 0)
        launch(plane, PIECES - 1 - piece, behind, 1)
    for piece in range(PIECES):
        launch(plane, piece, sibling, 4)
    for turn in range(PIECES):
        other = PIECES - 1 - turn
        came(behind, turn, 0)
        if turn < half:
            launch(behind, turn, ahead, 2)
        came(ahead, other, 1)
        if turn < half:
            launch(ahead, other, behind, 3)
        launch(behind, turn, sibling, 5)
        launch(ahead, other, sibling, 6)

    def collect(n, carry):
        source = target(n)
        pltpu.make_async_remote_copy(
            src_ref=solved.at[source, pl.ds(0, back_rows)], dst_ref=returned.at[source, pl.ds(0, back_rows)],
            send_sem=back_sem.at[source], recv_sem=home_sem.at[source], device_id=(source, plane), device_id_type=MESH,
        ).wait_recv()
        return carry

    lax.fori_loop(1, owners, collect, 0)
    returned[me, pl.ds(0, back_rows)] = solved[me, pl.ds(0, back_rows)]

    def unpack(b, carry):
        keeper = index_s[3, b]
        model_here = decode(
            returned[keeper, pl.ds(index_s[4, b], 1), :], returned[keeper, pl.ds(capacity, 1), :], MODEL_FRACTION
        )
        for part in range(2):
            residual_out[b, pl.ds(part, 1), :] = samples[b, pl.ds(part, 1), :] - model_here[part]
        return carry

    lax.fori_loop(0, blocks, unpack, 0, unroll=8)

    for turn in range(half):
        other = PIECES - 1 - turn
        came(opposite, turn, 2)
        launch(opposite, turn, sibling, 7)
        came(opposite, other, 3)
        launch(opposite, other, sibling, 7)

    def flip(which):
        return which + 1 - 2 * core

    share = coupling_v[pl.ds(plane, 1), :]
    number = lax.broadcasted_iota(jnp.int32, share.shape, 1)

    def term(which):
        part = jnp.sum(jnp.where(number == which, share, 0.0), axis=1, keepdims=True)
        return part * grids[which].astype(jnp.float32)

    coupled_out[...] = term(plane) + term(behind) + term(ahead) + term(opposite)
    for route, which in enumerate((sibling, flip(behind), flip(ahead), flip(opposite))):
        for piece in range(PIECES):
            came(which, piece, 4 + route)
    coupled_out[...] += term(sibling) + term(flip(behind)) + term(flip(ahead)) + term(flip(opposite))

    def settle(n):
        outward(n).wait_send()
        homeward(n).wait_send()

    each_partner(settle)
    for copy in started:
        copy.wait_send()


def body(visibilities, uv_cell, sub_pixel, w_plane, block_tile, model_grid, kernel_table, coupling):
    blocks = visibilities.shape[1]
    rows = visibilities.shape[3]
    owners = lax.axis_size("tile")
    capacity = 3 * blocks // owners
    tiles, side = model_grid.shape[1], model_grid.shape[2]
    oversample = kernel_table.shape[1]
    planes = lax.axis_size("freq")
    chips_x, chips_y = planes // 2, 4
    vmem = pl.BlockSpec(memory_space=pltpu.VMEM)
    hbm = pl.BlockSpec(memory_space=pltpu.HBM)
    copies = pltpu.SemaphoreType.DMA
    taps = (tiles * side, capacity * rows)
    operands = (
        block_tile,
        w_plane,
        coupling,
        visibilities[0],
        uv_cell[0],
        sub_pixel[0],
        model_grid.reshape(tiles * side, 2 * side),
        kernel_table.transpose(1, 2, 0),
    )
    residuals, coupled = pl.pallas_call(
        functools.partial(kernel, (owners, capacity, tiles, side, oversample, chips_y, chips_x)),
        out_shape=(
            jax.ShapeDtypeStruct((blocks, 2, rows), jnp.float32),
            jax.ShapeDtypeStruct((tiles * side, 2 * side), jnp.float32),
        ),
        in_specs=[hbm] * len(operands),
        out_specs=[vmem] * 2,
        scratch_shapes=[
            pltpu.SMEM((1, blocks), jnp.int32),
            pltpu.SMEM((1, blocks), jnp.int32),
            pltpu.VMEM((1, blocks), jnp.int32),
            pltpu.VMEM((planes, planes), jnp.float32),
            pltpu.VMEM((blocks, 2, rows), jnp.float32),
            pltpu.VMEM((blocks, 2, rows), jnp.int32),
            pltpu.VMEM((blocks, 2, rows), jnp.int32),
            pltpu.VMEM((tiles * side, 2 * side), jnp.bfloat16),
            pltpu.VMEM(operands[-1].shape, jnp.bfloat16),
            pltpu.VMEM((8, rows), jnp.float32),
            pltpu.VMEM((blocks + 1, 4, rows), jnp.int32),
            pltpu.VMEM((8, rows), jnp.int32),
            pltpu.SMEM((8, rows), jnp.int32),
            pltpu.VMEM((chips_y, 32, rows), jnp.float32),
            pltpu.VMEM((2 * side, tiles * side), jnp.bfloat16),
            pltpu.VMEM((owners, 40, rows), jnp.int32),
            pltpu.VMEM((owners, 40, rows), jnp.int32),
            pltpu.VMEM((owners, 16, rows), jnp.int32),
            pltpu.VMEM((owners, 16, rows), jnp.int32),
            pltpu.VMEM(taps, jnp.bfloat16),
            pltpu.VMEM(taps, jnp.bfloat16),
            pltpu.VMEM(taps, jnp.bfloat16),
            pltpu.VMEM(taps, jnp.bfloat16),
            pltpu.VMEM((tiles * side, 2 * side), jnp.float32),
            pltpu.VMEM((planes, tiles * side, 2 * side), jnp.bfloat16),
            copies((len(operands) + 1,)),
            copies,
            copies((owners,)),
            copies((owners,)),
            copies((owners,)),
            copies((owners,)),
            copies((8, PIECES)),
            copies((8, PIECES)),
        ],
        compiler_params=pltpu.CompilerParams(collective_id=0, has_side_effects=True, vmem_limit_bytes=40 << 20),
    )(*(pltpu.with_memory_space_constraint(operand, pltpu.HBM) for operand in operands))
    return residuals[None], coupled.reshape(1, tiles, side, 2 * side)


def solution(mesh):
    return jax.shard_map(
        body,
        mesh=mesh,
        in_specs=(
            P("freq", "tile", None, None),
            P("freq", "tile", None, None),
            P("freq", "tile", None, None),
            P("freq", "tile"),
            P("freq", "tile"),
            P("freq", "tile", None, None),
            P(),
            P(),
        ),
        out_specs=(P("freq", "tile", None, None), P("freq", "tile", None, None)),
        check_vma=False,
    )
```

time: 54.1 us -> 51.9 us (0.959)
  Pallas kernels: 52 us -> 49.8 us
    pallas_call x1, Pallas kernels: 52 us -> 49.8 us  [body(): pl.pallas_call(functools.partial(kernel, (owners, capacity, tiles, side,...]
where the time goes in v4:
time: 51.9 us; the launch traced here: 51.8 us
  Pallas kernels  49.8 us (96%)
  local copies, waits for them, and re-layouts  1.36 us (3%)
  between operations  0.64 us (1%)
    pallas_call x1, Pallas kernels, body(): pl.pallas_call(functools.partial(kernel, (owners, capacity, tiles, side,...  49.8 us
    unnamed x2, local copies, waits for them, and re-layouts  1.36 us

profile of v4, /device:TPU:1, one launch (start us, length us, event | category | flops | bytes accessed | tf_op | source)
XLA Modules:
  0.0 51.8 jit_solution(5939891034008253762)
XLA Ops:
  0.6 49.8 %shard_map.95 = (f32[128,2,128]{2,1,0:T(2,128)S(1)}, f32[256,256]{1,0:T(8,128)S(1)}) custom-call(s32[1,128]{1,0:T(1,128)} %tile_h.1, s32[1,128]{1,0:T(1,128)} %plane_h.1, f32[8,8]{1,0:T(8,128)} %coupling_h.1, f32[128,2,128]{2,1,0:T(2,128)} %bitcast.9, s32[128,2,128]{2,1,0:T(2,128)} %bitcast.10, s32[128,2,128]{2,1,0:T(2,128)} %bitcast.11, ...), custom_call_target="tpu_custom_call" | custom-call | tf_op jit(solution)/shard_map/pallas_call | solution.py:420
  50.5 0.7 %copy.12 = f32[1,128,2,128]{3,2,1,0:T(2,128)} copy(f32[1,128,2,128]{3,2,1,0:T(2,128)S(1)} %bitcast.8) | data formatting | bytes 262144
  51.1 0.7 %copy.13 = f32[1,2,128,256]{3,2,1,0:T(8,128)} copy(f32[1,2,128,256]{3,2,1,0:T(8,128)S(1)} %bitcast.7) | data formatting | bytes 524288

commit v5 on v4

--- a/solution.py
+++ b/solution.py
@@ -272,9 +272,11 @@
         )
 
     def chunk(n, turn, row, weighted, last_row, last_weighted):
+        add_grid(last_weighted, last_row)
+        work_chunk(got.at[origin(n)], model_t[...], table_ref[...], row, weighted, modelled.at[turn], capacity, side)
+
+    def seal(n, turn):
         source = origin(n)
-        add_grid(last_weighted, last_row)
-        work_chunk(got.at[source], model_t[...], table_ref[...], row, weighted, modelled.at[turn], capacity, side)
         real, imaginary = modelled[turn, pl.ds(0, capacity), :], modelled[turn, pl.ds(16, capacity), :]
         here = measure(jnp.maximum(jnp.abs(real), jnp.abs(imaginary)), MODEL_FRACTION)
         solved[source, pl.ds(0, capacity), :] = encode(
@@ -282,23 +284,32 @@
         )
         solved[source, pl.ds(capacity, 1), :] = jnp.broadcast_to(here, (1, lanes))
 
+    late = chips_y - 1
+    modelled[late] = jnp.zeros_like(modelled[late])
+
     def group(step, carry):
         first = chips_y * step
         for across in range(chips_y):
             arrival(first + across).wait_recv()
+        seal(lax.rem(first + owners - 1, owners), late)
         for across in range(0, chips_y, 2):
             chunk(first + across, across, row0, weighted0, row1, weighted1)
             chunk(first + across + 1, across + 1, row1, weighted1, row0, weighted0)
+        for across in range(late):
+            seal(first + across, across)
 
         @pl.when(step > 0)
         def _():
+            homeward(first - 1).start()
             homeward(first).start()
 
-        for across in range(1, chips_y):
+        for across in range(1, late):
             homeward(first + across).start()
         return carry
 
     lax.fori_loop(0, chips_z, group, 0)
+    seal(owners - 1, late)
+    homeward(owners - 1).start()
     add_grid(weighted1, row1)
 
     piece_rows = tiles * side // PIECES

time: 51.9 us -> 51.5 us (level)
  no operation moved by 1% of the time
where the time goes in v5:
time: 51.5 us; the launch traced here: 51.4 us
  Pallas kernels  49.4 us (96%)
  local copies, waits for them, and re-layouts  1.36 us (3%)
  between operations  0.64 us (1%)
    pallas_call x1, Pallas kernels, body(): pl.pallas_call(functools.partial(kernel, (owners, capacity, tiles, side,...  49.4 us
    unnamed x2, local copies, waits for them, and re-layouts  1.36 us

profile of v5, /device:TPU:1, one launch (start us, length us, event | category | flops | bytes accessed | tf_op | source)
XLA Modules:
  0.0 51.4 jit_solution(3591710780441740976)
XLA Ops:
  0.6 49.4 %shard_map.95 = (f32[128,2,128]{2,1,0:T(2,128)S(1)}, f32[256,256]{1,0:T(8,128)S(1)}) custom-call(s32[1,128]{1,0:T(1,128)} %tile_h.1, s32[1,128]{1,0:T(1,128)} %plane_h.1, f32[8,8]{1,0:T(8,128)} %coupling_h.1, f32[128,2,128]{2,1,0:T(2,128)} %bitcast.9, s32[128,2,128]{2,1,0:T(2,128)} %bitcast.10, s32[128,2,128]{2,1,0:T(2,128)} %bitcast.11, ...), custom_call_target="tpu_custom_call" | custom-call | tf_op jit(solution)/shard_map/pallas_call | solution.py:431
  50.0 0.7 %copy.12 = f32[1,128,2,128]{3,2,1,0:T(2,128)} copy(f32[1,128,2,128]{3,2,1,0:T(2,128)S(1)} %bitcast.8) | data formatting | bytes 262144
  50.7 0.7 %copy.13 = f32[1,2,128,256]{3,2,1,0:T(8,128)} copy(f32[1,2,128,256]{3,2,1,0:T(8,128)S(1)} %bitcast.7) | data formatting | bytes 524288
